TPU v7x, 32 devices: a whole 2x2x4 slice. The times are simulated.
32 devices in a mesh: dp: 8 (over y, x, core), seq: 4 (over z).
Axes of the slice: x: 2, y: 2, z: 4, core: 2. Of those that a mesh axis runs over, the one named last changes fastest.
Arguments:
- inputs: bfloat16 [8, 3072, 768], P('dp', 'seq'), may hold values from -6 to 6
- pass_embed: bfloat16 [768], P('dp'), may hold values from -3 to 3
- gain_attend: bfloat16 [768], P('dp'), may hold values from 0.25 to 1.75
- shift_attend: bfloat16 [768], P('dp'), may hold values from -3 to 3
- attend_in: bfloat16 [768, 2304], P('dp'), may hold values from -0.21875 to 0.21875
- attend_out: bfloat16 [768, 768], P('dp'), may hold values from -0.875 to 0.875
- gain_hidden: bfloat16 [768], P('dp'), may hold values from 0.25 to 1.75
- shift_hidden: bfloat16 [768], P('dp'), may hold values from -3 to 3
- hidden_up: bfloat16 [768, 3072], P('dp'), may hold values from -0.21875 to 0.21875
- hidden_down: bfloat16 [3072, 768], P('dp'), may hold values from -0.109375 to 0.109375
- cotangent: bfloat16 [8, 3072, 768], P('dp', 'seq'), may hold values from -6 to 6
Outputs:
- layer_out: bfloat16 [8, 3072, 768], P('dp', 'seq')
- input_grad: float32 [8, 3072, 768], P('dp', 'seq')
- embed_grad: float32 [768], P('dp')
- gain_attend_grad: float32 [768], P('dp')
- shift_attend_grad: float32 [768], P('dp')
- attend_in_grad: float32 [768, 2304], P('dp')
- attend_out_grad: float32 [768, 768], P('dp')
- gain_hidden_grad: float32 [768], P('dp')
- shift_hidden_grad: float32 [768], P('dp')
- hidden_up_grad: float32 [768, 3072], P('dp')
- hidden_down_grad: float32 [3072, 768], P('dp')
All inputs are finite; a program needn't handle non-finite values.
Results may differ from a plain program's by a relative error of at most 0.007.
Values may be sent and summed in bfloat16 or wider, within the bound.
No kernel may reach another device: no remote copies, remote signals or barrier semaphores. Data moves between devices by JAX's collectives and lax.ppermute only.
A program may use at most 192 MiB of HBM per device.

v0:
```python
import functools

import jax
import jax.numpy as jnp
from jax import lax
from jax.experimental import pallas as pl
from jax.experimental.pallas import tpu as pltpu
from jax.sharding import PartitionSpec as P

HD = 64
EPSILON = 1e-05
MASKED = -1e30
F32 = jnp.float32
BF = jnp.bfloat16
MEMBERS = 4
VMEM_LIMIT = 60 << 20
GELU_A = 0.7978845608028654
GELU_B = 0.044715


def contract(left, right, left_dim, right_dim):
    return lax.dot_general(
        left, right, (((left_dim,), (right_dim,)), ((), ())), preferred_element_type=F32
    )


def normalize(hidden):
    center = hidden - jnp.mean(hidden, axis=-1, keepdims=True)
    spread = jnp.mean(center * center, axis=-1, keepdims=True)
    inverse = lax.rsqrt(spread + EPSILON)
    return center * inverse, inverse


def norm_backward(grad, gain, unit, inverse):
    scaled = grad * gain
    return inverse * (
        scaled
        - jnp.mean(scaled, axis=-1, keepdims=True)
        - unit * jnp.mean(scaled * unit, axis=-1, keepdims=True)
    )


def params(*semantics):
    return pltpu.CompilerParams(dimension_semantics=semantics, vmem_limit_bytes=VMEM_LIMIT)


def whole(shape):
    zeros = (0,) * len(shape)
    return pl.BlockSpec(shape, lambda *_: zeros, pipeline_mode=pl.Buffered(1))


def project_body(count, info, *refs):
    sources, wt = refs[: 2 * count], refs[2 * count]
    packed, normed = refs[-2:]
    slot = pl.program_id(0)
    stay = info[0] > 0
    cols = wt.shape[0] - 64
    vec = wt[cols : cols + 8, :].astype(F32)
    for which in range(count):
        for wanted in (True, False):
            source = sources[2 * which + (0 if wanted else 1)]

            @pl.when(jnp.logical_and(slot == which, stay == wanted))
            def _(source=source):
                unit, _ = normalize(source[...].astype(F32) + vec[0:1])
                normed[...] = (unit * vec[1:2] + vec[2:3]).astype(BF)

    packed[...] = contract(wt[:cols, :], normed[...], 1, 1).astype(BF)


def project(info, sources, wt, carried, rows=384):
    chunk, width = sources[0].shape
    count = len(sources) // 2
    cols = wt.shape[0] - 64
    length = MEMBERS * chunk
    per = chunk // rows

    def src(which, wanted):
        def index(s, b, info):
            block = jnp.where(s == which, b, (per - 1) * (s > which))
            return (jnp.where(info[0] == wanted, block, 0), 0)

        return pl.BlockSpec((rows, width), index)

    def place(s, b, info):
        return info[1 + s] * per + b

    in_specs = [src(w, f) for w in range(count) for f in (1, 0)] + [whole(wt.shape)]
    aliases = {}
    args = [info, *sources, wt]
    if carried is not None:
        in_specs += [pl.BlockSpec(memory_space=pl.ANY)] * 2
        aliases = {2 * count + 2: 0, 2 * count + 3: 1}
        args += list(carried)
    return pl.pallas_call(
        functools.partial(project_body, count),
        grid_spec=pltpu.PrefetchScalarGridSpec(
            num_scalar_prefetch=1,
            grid=(count, per),
            in_specs=in_specs,
            out_specs=[
                pl.BlockSpec((cols, rows), lambda s, b, info: (0, place(s, b, info))),
                pl.BlockSpec((rows, width), lambda s, b, info: (place(s, b, info), 0)),
            ],
        ),
        out_shape=[
            jax.ShapeDtypeStruct((cols, length), BF),
            jax.ShapeDtypeStruct((length, width), BF),
        ],
        input_output_aliases=aliases,
        compiler_params=params("arbitrary", "arbitrary"),
        cost_estimate=pl.CostEstimate(
            flops=2 * count * chunk * width * cols,
            transcendentals=count * chunk,
            bytes_accessed=6 * count * chunk * width,
        ),
        name="norm_project",
    )(*args)


def diagonal(size):
    key = lax.broadcasted_iota(jnp.int32, (size, size), 0)
    query = lax.broadcasted_iota(jnp.int32, (size, size), 1)
    return key <= query


def forward_body(heads, info, packed, out0, out1, out2, out3, logsum, keys):
    step = pl.program_id(0)
    width = heads * HD
    size = out0.shape[1]
    scale = BF(HD**-0.5)

    @pl.when(step == 0)
    def _():
        for h in range(heads):
            keys[h] = packed[width + h * HD : width + (h + 1) * HD, :].T

    first = pl.multiple_of(step * size, size)
    queries = [packed[h * HD : (h + 1) * HD, pl.ds(first, size)] * scale for h in range(heads)]

    def block(span, carry, allowed, part):
        all_scores = [
            contract(keys[h, span, :], queries[h][:, part], 1, 0) for h in range(heads)
        ]
        result = []
        for h in range(heads):
            top, total, summed = carry[h]
            scores = all_scores[h]
            if allowed is not None:
                scores = jnp.where(allowed, scores, MASKED)
            new_top = jnp.maximum(top, jnp.max(scores, axis=0, keepdims=True))
            weights = jnp.exp(scores - new_top)
            shrink = jnp.exp(top - new_top)
            total = total * shrink + jnp.sum(weights, axis=0, keepdims=True)
            values = packed[2 * width + h * HD : 2 * width + (h + 1) * HD, span]
            summed = summed * shrink + contract(values, weights.astype(BF), 1, 0)
            result.append((new_top, total, summed))
        return tuple(result)

    begin = tuple(
        (
            jnp.full((1, size), MASKED, F32),
            jnp.zeros((1, size), F32),
            jnp.zeros((HD, size), F32),
        )
        for _ in range(heads)
    )
    carry = lax.fori_loop(
        0,
        step,
        lambda j, c: block(pl.ds(pl.multiple_of(j * size, size), size), c, None, slice(0, size)),
        begin,
    )
    half = size // 2
    lower, upper = pl.ds(first, half), pl.ds(pl.multiple_of(first + half, half), half)
    allowed = diagonal(half)
    left = [tuple(v[:, :half] for v in c) for c in carry]
    right = [tuple(v[:, half:] for v in c) for c in carry]
    left = block(lower, left, allowed, slice(0, half))
    right = block(lower, right, None, slice(half, size))
    right = block(upper, right, allowed, slice(half, size))
    carry = [
        tuple(jnp.concatenate([a, b], axis=1) for a, b in zip(l, r)) for l, r in zip(left, right)
    ]
    place = step ^ info[1]
    for h in range(heads):
        top, total, summed = carry[h]
        logsum[h : h + 1, :] = top + jnp.log(total)
        low = (summed / total).astype(BF)
        for j, out in enumerate((out0, out1, out2, out3)):

            @pl.when(place == j)
            def _(out=out, low=low, h=h):
                out[h * HD : (h + 1) * HD, :] = low


def attend_forward(info, packed):
    cols, length = packed.shape
    heads = cols // (3 * HD)
    width = heads * HD
    size = length // MEMBERS
    part = jax.ShapeDtypeStruct((width, size), BF)
    return pl.pallas_call(
        functools.partial(forward_body, heads),
        grid_spec=pltpu.PrefetchScalarGridSpec(
            num_scalar_prefetch=1,
            grid=(MEMBERS,),
            in_specs=[whole(packed.shape)],
            out_specs=[pl.BlockSpec((width, size), lambda s, info: (0, 0))] * MEMBERS
            + [pl.BlockSpec((8, size), lambda s, info: (0, s))],
            scratch_shapes=[pltpu.VMEM((heads, length, HD), BF)],
        ),
        out_shape=[part] * MEMBERS + [jax.ShapeDtypeStruct((8, length), F32)],
        compiler_params=params("arbitrary"),
        cost_estimate=pl.CostEstimate(
            flops=heads * length * HD, transcendentals=length, bytes_accessed=width * length
        ),
        name="attention_forward",
    )(info, packed)


def backward_body(heads, top, info, packed, o0, o1, o2, o3, g0, g1, g2, g3, logsum, wt, *rest):
    last_stage = top == 1
    keys, values, grad_keys, grad_values, out_all, grad_all = rest[-6:]
    if last_stage:
        keys_in, values_in, near, far, stacked_out = rest[:-6]
    else:
        near, far, stacked_out, keys_out, values_out = rest[:-6]
    step = pl.program_id(0)
    chunk_id = top - step
    width = heads * HD
    size = near.shape[0]
    scale = BF(HD**-0.5)

    @pl.when(step == 0)
    def _():
        for h in range(heads):
            keys[h] = packed[width + h * HD : width + (h + 1) * HD, :].T
            values[h] = packed[2 * width + h * HD : 2 * width + (h + 1) * HD, :].T
        if last_stage:
            grad_keys[...] = keys_in[...]
            grad_values[...] = values_in[...]
        else:
            grad_keys[...] = jnp.zeros_like(grad_keys)
            grad_values[...] = jnp.zeros_like(grad_values)
        for j, (o, g) in enumerate(((o0, g0), (o1, g1), (o2, g2), (o3, g3))):
            out_all[info[1] ^ j] = o[...]
            grad_all[info[1] ^ j] = g[...]

    first = pl.multiple_of(chunk_id * size, size)
    rows = [slice(h * HD, (h + 1) * HD) for h in range(heads)]
    query_t = [packed[r, pl.ds(first, size)] * scale for r in rows]
    query = [q.T for q in query_t]
    grad_t = [grad_all[chunk_id, r, :] for r in rows]
    grad = [g.T for g in grad_t]
    delta = [
        jnp.sum(g.astype(F32) * out_all[chunk_id, r, :].astype(F32), axis=0, keepdims=True)
        for g, r in zip(grad_t, rows)
    ]
    lse = [logsum[h : h + 1, :] for h in range(heads)]

    def block(span, carry, allowed, part):
        result = []
        for h in range(heads):
            scores = contract(keys[h, span, :], query_t[h][:, part], 1, 0)
            grad_probs = contract(values[h, span, :], grad_t[h][:, part], 1, 0)
            probs = jnp.exp(scores - lse[h][:, part])
            if allowed is not None:
                probs = jnp.where(allowed, probs, 0.0)
            grad_scores = (probs * (grad_probs - delta[h][:, part])).astype(BF)
            grad_values[h, span, :] += contract(probs.astype(BF), grad[h][part], 1, 0)
            grad_keys[h, span, :] += contract(grad_scores, query[h][part], 1, 0)
            keys_t = packed[width + h * HD : width + (h + 1) * HD, span]
            result.append(carry[h] + contract(keys_t, grad_scores, 1, 0))
        return tuple(result)

    grad_query = tuple(jnp.zeros((HD, size), F32) for _ in range(heads))
    grad_query = lax.fori_loop(
        0,
        chunk_id,
        lambda j, c: block(pl.ds(pl.multiple_of(j * size, size), size), c, None, slice(0, size)),
        grad_query,
    )
    half = size // 2
    lower, upper = pl.ds(first, half), pl.ds(pl.multiple_of(first + half, half), half)
    allowed = diagonal(half)
    left = block(lower, [g[:, :half] for g in grad_query], allowed, slice(0, half))
    right = block(lower, [g[:, half:] for g in grad_query], None, slice(half, size))
    right = block(upper, right, allowed, slice(half, size))
    grad_query = [jnp.concatenate([a, b], axis=1) for a, b in zip(left, right)]
    pieces = [(g * HD**-0.5).astype(BF) for g in grad_query]
    pieces += [grad_keys[h, pl.ds(first, size), :].astype(BF).T for h in range(heads)]
    pieces += [grad_values[h, pl.ds(first, size), :].astype(BF).T for h in range(heads)]
    stacked = jnp.concatenate(pieces, axis=0)
    partial = contract(stacked, wt[: 3 * width, :], 0, 0).astype(BF)
    is_near = ((chunk_id ^ info[1]) & 1) == 0

    @pl.when(is_near)
    def _():
        near[...] = partial

    @pl.when(jnp.logical_not(is_near))
    def _():
        far[...] = partial

    stacked_out[...] = stacked
    if not last_stage:

        @pl.when(step == 1)
        def _():
            left = keys_out.shape[1]
            keys_out[...] = grad_keys[:, :left, :]
            values_out[...] = grad_values[:, :left, :]


def attend_backward(info, packed, outs, grads, logsum, wt, carried=None):
    cols, length = packed.shape
    heads = cols // (3 * HD)
    width = heads * HD
    size = length // MEMBERS
    model = wt.shape[1]
    top = MEMBERS - 1 if carried is None else 1
    span = (top + 1) * size
    left = length // 2

    def fixed(shape):
        zeros = (0,) * len(shape)
        return pl.BlockSpec(shape, lambda s, info: zeros)

    partial = jax.ShapeDtypeStruct((size, model), BF)
    state = jax.ShapeDtypeStruct((heads, left, HD), F32)
    in_specs = (
        [whole((cols, span))]
        + [whole((width, size))] * (2 * MEMBERS)
        + [
            pl.BlockSpec((8, size), lambda s, info: (0, top - s)),
            whole(wt.shape),
        ]
    )
    out_shape = [partial, partial, jax.ShapeDtypeStruct((cols, 2 * size), BF)]
    out_specs = [fixed((size, model))] * 2
    out_specs += [pl.BlockSpec((cols, size), lambda s, info: (0, 1 - s))]
    if carried is None:
        more = ()
        out_shape += [state, state]
        out_specs += [fixed(state.shape)] * 2
    else:
        more = tuple(carried)
        in_specs += [whole(state.shape)] * 2
    blocks = 7 if carried is None else 3
    return pl.pallas_call(
        functools.partial(backward_body, heads, top),
        grid_spec=pltpu.PrefetchScalarGridSpec(
            num_scalar_prefetch=1,
            grid=(2,),
            in_specs=in_specs,
            out_specs=out_specs,
            scratch_shapes=[
                pltpu.VMEM((heads, span, HD), BF),
                pltpu.VMEM((heads, span, HD), BF),
                pltpu.VMEM((heads, span, HD), F32),
                pltpu.VMEM((heads, span, HD), F32),
                pltpu.VMEM((MEMBERS, width, size), BF),
                pltpu.VMEM((MEMBERS, width, size), BF),
            ],
        ),
        out_shape=out_shape,
        compiler_params=params("arbitrary"),
        cost_estimate=pl.CostEstimate(
            flops=200 * heads * blocks * size * size * HD,
            transcendentals=heads * blocks * size * size,
            bytes_accessed=20 * width * length,
        ),
        name="attention_backward",
    )(info, packed, *outs, *grads, logsum, wt, *more)


def project_grad_body(*refs):
    stacked, normed = refs[:2]
    out, total = refs[-2:]
    step = pl.program_id(0)
    part = contract(stacked[...], normed[...], 1, 0)

    @pl.when(step == 0)
    def _():
        total[...] = part if len(refs) == 4 else refs[2][...] + part

    @pl.when(step == 1)
    def _():
        if len(refs) == 4:
            out[...] = total[...] + part
        else:
            out[...] = (total[...] + part).astype(BF).T


def project_grad(stacked, normed, half, before=None):
    cols, span = stacked.shape
    size = span // 2
    model = normed.shape[1]
    more = () if before is None else (before,)
    if before is None:
        out = jax.ShapeDtypeStruct((cols, model), F32)
    else:
        out = jax.ShapeDtypeStruct((model, cols), BF)
    return pl.pallas_call(
        project_grad_body,
        grid=(2,),
        in_specs=[
            pl.BlockSpec((cols, size), lambda s: (0, s)),
            pl.BlockSpec((size, model), lambda s: (2 * half + s, 0)),
        ]
        + [whole((cols, model))] * len(more),
        out_specs=pl.BlockSpec(out.shape, lambda s: (0, 0)),
        out_shape=out,
        scratch_shapes=[pltpu.VMEM((cols, model), F32)],
        compiler_params=params("arbitrary"),
        cost_estimate=pl.CostEstimate(
            flops=2 * cols * span * model, transcendentals=0, bytes_accessed=2 * span * (cols + model)
        ),
        name="project_grad",
    )(stacked, normed, *more)


def hidden_body(groups, rows, info, tok, cot, m0, m1, m2, m3, vec_ref, down_ref, up_ref, out_w, *rest):
    (
        layer_out, resid_grad, a0, a1, a2, a3, stats, down_own, down_other, grads,
        low, unit, inverse, result, grad_n, act, grad_pre, stage, sems,
    ) = rest
    step = pl.program_id(0)
    member = info[1]
    vec = vec_ref[0:8, :].astype(F32)
    size, model = tok.shape
    width = model // MEMBERS
    units, piece = stage.shape[1], stage.shape[2]
    split = grads.shape[0]
    share = units // MEMBERS

    def out_rows(j):
        if split == 1:
            return out_w[0, pl.ds(pl.multiple_of((member ^ j) * width, width), width), :]
        unit_rows = out_w.shape[1]
        count = width // unit_rows
        return out_w[pl.ds((member ^ j) * count, count)].reshape(width, model)

    def drain(slot):
        pltpu.make_async_copy(stage.at[slot], stage.at[slot], sems.at[slot]).wait()

    def put_down(slot, block):
        for b in range(units):
            source = stage.at[slot, b]
            if split == 1:
                start = pl.multiple_of(block * model + b * piece, 16)
                target = down_own.at[0, pl.ds(start, piece), :]
                pltpu.make_async_copy(source, target, sems.at[slot]).start()
                continue
            per = units // 2
            rows_at = slice((b % per) * piece, (b % per + 1) * piece)
            for wanted, array in ((True, down_own), (False, down_other)):

                @pl.when((info[2] == b // per) == wanted)
                def _(array=array, source=source, rows_at=rows_at):
                    target = array.at[block, rows_at, :]
                    pltpu.make_async_copy(source, target, sems.at[slot]).start()

    def put(slot, block):
        for b in range(units):
            if split == 1:
                row, start = 0, block * model + b * piece
            else:
                row, start = b, block * piece
            if not isinstance(start, int):
                start = pl.multiple_of(start, 16)
            pltpu.make_async_copy(
                stage.at[slot, b], grads.at[row, pl.ds(start, piece), :], sems.at[slot]
            ).start()

    @pl.when(step == 0)
    def _():
        branch = None
        for j, merged in enumerate((m0, m1, m2, m3)):
            part = contract(merged[...], out_rows(j), 0, 0)
            branch = part if branch is None else branch + part
        resid = tok[...].astype(F32) + vec[0:1] + branch
        normal, spread = normalize(resid)
        low[...] = (normal * vec[3:4] + vec[4:5]).astype(BF)
        unit[...] = normal
        inverse[...] = spread
        result[...] = resid
        grad_n[...] = jnp.zeros_like(grad_n)

    up = up_ref[...].reshape(model, model)
    down = down_ref[...].reshape(model, model)

    def tile(i, _):
        span = pl.ds(pl.multiple_of(i * rows, rows), rows)
        pre = contract(low[span, :], up, 1, 0)
        grad_act = contract(cot[span, :], down, 1, 1)
        square = pre * pre
        half = 0.5 + 0.5 * jnp.tanh(pre * (GELU_A + GELU_A * GELU_B * square))
        gelu = pre * half
        act_low = gelu.astype(BF)
        act[span, :] = act_low
        slope = half + gelu * (1.0 - half) * (2.0 * GELU_A + 6.0 * GELU_A * GELU_B * square)
        grad_low = (grad_act * slope).astype(BF)
        grad_pre[span, :] = grad_low
        result[span, :] += contract(act_low, down, 1, 0)
        grad_n[span, :] += contract(grad_low, up, 1, 1)
        return 0

    if rows == size:
        tile(0, 0)
    else:
        lax.fori_loop(0, size // rows, tile, 0)

    slot = 2 * (step % 2)

    @pl.when(step >= 2)
    def _():
        drain(slot)
        drain(slot + 1)

    stage[slot] = contract(act[...], cot[...], 0, 0).astype(BF).reshape(units, piece, model)
    put_down(slot, step)
    stage[slot + 1] = contract(low[...], grad_pre[...], 0, 0).astype(BF).reshape(units, piece, model)
    put(slot + 1, step)

    @pl.when(step == groups - 1)
    def _():
        layer_out[...] = result[...].astype(BF)
        grad = grad_n[...]
        total = cot[...].astype(F32) + norm_backward(grad, vec[3:4], unit[...], inverse[...])
        resid_grad[...] = total
        branch = total.astype(BF)
        for j, out in enumerate((a0, a1, a2, a3)):
            out[...] = contract(out_rows(j), branch, 1, 1).astype(BF)
        stats[...] = jnp.zeros_like(stats)
        stats[0:1, :] = jnp.sum(grad * unit[...], axis=0, keepdims=True)
        stats[1:2, :] = jnp.sum(grad, axis=0, keepdims=True)
        other = 2 * (groups % 2)
        drain(other)
        for j, merged in enumerate((m0, m1, m2, m3)):
            block = contract(merged[...], branch, 1, 0).astype(BF)
            stage[other, pl.ds((member ^ j) * share, share)] = block.reshape(share, piece, model)
        put(other, groups)
        for which in range(4):
            drain(which)


def hidden_layer(info, tok, cot, merged, wt, weights, groups, rows=768):
    size, model = tok.shape
    width = model // MEMBERS
    split, height, _ = weights.shape
    unit = model // split
    tall = height - (groups + 1) * unit
    units = 8
    vec_block = wt.shape[0] // 64 - 1
    down_shape = (1, tall, model) if split == 1 else (split // 2, tall, model)
    if split == 1:
        down_spec = pl.BlockSpec((1, model, model), lambda k, info: (0, k, 0))
        up_spec = pl.BlockSpec((1, model, model), lambda k, info: (0, groups + k, 0))
        out_spec = pl.BlockSpec(
            (1, model, model), lambda k, info: (0, 2 * groups, 0), pipeline_mode=pl.Buffered(1)
        )
    else:
        base = tall // unit
        down_spec = pl.BlockSpec((model // tall, tall, model), lambda k, info: (k, 0, 0))
        up_spec = pl.BlockSpec((split, unit, model), lambda k, info: (0, base + k, 0))
        out_spec = pl.BlockSpec(
            (split, unit, model),
            lambda k, info: (0, base + groups, 0),
            pipeline_mode=pl.Buffered(1),
        )

    def fixed(shape):
        zeros = (0,) * len(shape)
        return pl.BlockSpec(shape, lambda k, info: zeros)

    def shaped(shape, dtype):
        return jax.ShapeDtypeStruct(shape, dtype)

    return pl.pallas_call(
        functools.partial(hidden_body, groups, rows),
        grid_spec=pltpu.PrefetchScalarGridSpec(
            num_scalar_prefetch=1,
            grid=(groups,),
            in_specs=[whole((size, model))] * 2
            + [whole((width, size))] * MEMBERS
            + [
                pl.BlockSpec((64, model), lambda k, info: (vec_block, 0)),
                down_spec,
                up_spec,
                out_spec,
            ],
            out_specs=[fixed((size, model))] * 2
            + [fixed((width, size))] * MEMBERS
            + [fixed((8, model))]
            + [pl.BlockSpec(memory_space=pl.ANY)] * 3,
            scratch_shapes=[
                pltpu.VMEM((size, model), BF),
                pltpu.VMEM((size, model), F32),
                pltpu.VMEM((size, 1), F32),
                pltpu.VMEM((size, model), F32),
                pltpu.VMEM((size, model), F32),
                pltpu.VMEM((size, model), BF),
                pltpu.VMEM((size, model), BF),
                pltpu.VMEM((4, units, model // units, model), BF),
                pltpu.SemaphoreType.DMA((4,)),
            ],
        ),
        out_shape=[shaped((size, model), BF), shaped((size, model), F32)]
        + [shaped((width, size), BF)] * MEMBERS
        + [
            shaped((8, model), F32),
            shaped(down_shape, BF),
            shaped(down_shape if split > 1 else (1, 16, model), BF),
            shaped((split, (groups + 1) * unit, model), BF),
        ],
        compiler_params=params("arbitrary"),
        cost_estimate=pl.CostEstimate(
            flops=6 * size * model * (2 * groups + 1) * model,
            transcendentals=size * groups * model,
            bytes_accessed=4 * weights.size + 12 * size * model,
        ),
        name="hidden_layer",
    )(info, tok, cot, *merged, wt, weights, weights, weights)


def final_body(owner, info, tok, p0, p1, p2, resid_grad, vec_ref, before, *rest):
    out, low, stats = rest[-3:]
    step = pl.program_id(0)
    mine = info[2] == owner
    vec = vec_ref[0:8, :].astype(F32)

    @pl.when(step == 0)
    def _():
        stats[...] = before[...]

    @pl.when(mine)
    def _():
        unit, inverse = normalize(tok[...].astype(F32) + vec[0:1])
        grad = p0[...].astype(F32) + p1[...].astype(F32) + p2[...].astype(F32)
        result = resid_grad[...] + norm_backward(grad, vec[1:2], unit, inverse)
        out[...] = result
        low[...] = result.astype(BF)
        stats[2:3, :] += jnp.sum(grad * unit, axis=0, keepdims=True)
        stats[3:4, :] += jnp.sum(grad, axis=0, keepdims=True)
        stats[4:5, :] += jnp.sum(result, axis=0, keepdims=True)

    if len(rest) == 4:

        @pl.when(jnp.logical_not(mine))
        def _():
            out[...] = rest[0][...]


def final_norm(owner, info, tokens, parts, resid_grad, wt, before, earlier=None, rows=384):
    size, model = tokens.shape
    tok = pl.BlockSpec((rows, model), lambda s, info: (s, 0))
    one = pl.BlockSpec((8, model), lambda s, info: (0, 0))
    vec_block = wt.shape[0] // 64 - 1
    more = () if earlier is None else (earlier,)
    return pl.pallas_call(
        functools.partial(final_body, owner),
        grid_spec=pltpu.PrefetchScalarGridSpec(
            num_scalar_prefetch=1,
            grid=(size // rows,),
            in_specs=[tok] * 5
            + [pl.BlockSpec((64, model), lambda s, info: (vec_block, 0)), one]
            + [tok] * len(more),
            out_specs=[tok, tok, one],
        ),
        out_shape=[
            jax.ShapeDtypeStruct((size, model), F32),
            jax.ShapeDtypeStruct((size, model), BF),
            jax.ShapeDtypeStruct((8, model), F32),
        ],
        compiler_params=params("arbitrary"),
        cost_estimate=pl.CostEstimate(
            flops=size * model, transcendentals=size, bytes_accessed=size * model
        ),
        name="final_norm",
    )(info, tokens, *parts, resid_grad, wt, before, *more)


def together(*values):
    return lax.optimization_barrier(values)


def on_device(
    groups_dp,
    inputs,
    pass_embed,
    gain_attend,
    shift_attend,
    attend_in,
    attend_out,
    gain_hidden,
    shift_hidden,
    hidden_up,
    hidden_down,
    cotangent,
):
    axes = ("dp", "seq")
    dp = groups_dp
    row = lax.axis_index("dp")
    line = lax.axis_index("seq")
    core = row & 1
    stays = core == (line >> 1)
    member = core * 2 + (line & 1)
    model = inputs.shape[2]
    width = model // MEMBERS
    share = attend_in.shape[0]
    groups = hidden_up.shape[1] // model

    def send(value, target):
        pairs = []
        for d in range(dp):
            for z in range(MEMBERS):
                goal = target(d, z)
                if goal is not None:
                    pairs.append((d * MEMBERS + z, goal[0] * MEMBERS + goal[1]))
        return lax.ppermute(value, axes, pairs)

    def at_home(d, z):
        return (d & 1) == (z >> 1)

    def swap(d, z):
        return None if at_home(d, z) else (d ^ 1, z ^ 2)

    def other_core(d, z):
        return (d ^ 1, z)

    def next_chip(d, z):
        return (d, z ^ 1)

    mine = inputs[0]
    first = send(mine, lambda d, z: (d, z ^ 1) if at_home(d, z) else (d ^ 1, z ^ 2))
    mine_other = send(mine, other_core)

    columns = attend_in.reshape(share, 3, MEMBERS, width).transpose(2, 0, 1, 3)
    columns = columns.reshape(MEMBERS, share, 3 * width)
    vectors = jnp.stack([pass_embed, gain_attend, shift_attend, gain_hidden, shift_hidden], axis=1)
    vectors = jnp.pad(vectors, ((0, 0), (0, 59)))

    def for_member(which):
        piece = lax.dynamic_index_in_dim(columns, which, 0, keepdims=False)
        return jnp.concatenate([piece, vectors], axis=1)

    def ordered(which, low_piece, high_piece):
        return jnp.where(
            which,
            jnp.concatenate([high_piece, low_piece]),
            jnp.concatenate([low_piece, high_piece]),
        )

    def is_upper(bit):
        return ((row >> bit) & 1) == 1

    def flipped(mask):
        return lambda d, z: (d ^ mask, z)

    bits = dp.bit_length() - 1
    own = for_member(member)[None]
    gathered = ordered(is_upper(0), own, send(for_member(member ^ 2), other_core)[None])
    bit = 1
    while bit < bits:
        near = ordered(is_upper(bit), gathered, send(gathered, flipped(1 << bit)))
        if bit + 1 < bits:
            far = ordered(
                is_upper(bit),
                send(gathered, flipped(2 << bit)),
                send(gathered, flipped(3 << bit)),
            )
            near = ordered(is_upper(bit + 1), near, far)
        gathered = near
        bit += 2
    first, gathered = together(first, gathered)
    wt = gathered.reshape(model, 3 * width + 64).T
    late = send(first, lambda d, z: None if at_home(d, z) else (d, z ^ 1))
    first_other = send(first, other_core)

    pack = jnp.concatenate(
        [hidden_down]
        + [hidden_up[:, k * model : (k + 1) * model] for k in range(groups)]
        + [attend_out]
    )
    height = pack.shape[0]
    weights = lax.all_gather(pack, "dp", axis=0, tiled=False)
    split = dp if (model // dp) % 96 == 0 else 1
    if split == 1:
        tall = hidden_down.shape[0]
        down = weights[:, :tall].reshape(1, dp * tall, model)
        others = weights[:, tall:].reshape(dp, groups + 1, share, model).transpose(1, 0, 2, 3)
        weights = jnp.concatenate([down, others.reshape(1, -1, model)], axis=1)

    stay_flag = stays.astype(jnp.int32)
    early = jnp.where(stays, member, member ^ 2)
    info = jnp.stack([stay_flag, member, core]).astype(jnp.int32)
    info_early = jnp.stack([stay_flag, early, early ^ 1, early ^ 2]).astype(jnp.int32)
    info_late = jnp.stack([stay_flag, early ^ 3]).astype(jnp.int32)
    carried = project(
        info_early, [mine, mine_other, first, first_other, first_other, first], wt, None
    )
    late, packed, grad_mine = together(late, carried[0], cotangent[0])
    late_other = send(late, other_core)
    packed, normed = project(info_late, [late_other, late], wt, [packed, carried[1]])
    grad_moved = send(grad_mine, swap)

    *outs, logsum = attend_forward(info, packed)
    mine, first, logsum = together(mine, first, logsum)
    routes = [None, next_chip, other_core, lambda d, z: (d ^ 1, z ^ 1)]
    merged = [outs[0]] + [send(outs[j], routes[j]) for j in (1, 3, 2)]
    merged = [merged[0], merged[1], merged[3], merged[2]]

    tokens = jnp.where(stays, mine, first)
    cot = jnp.where(stays, grad_mine, grad_moved)
    layer_out, resid_grad, a0, a1, a2, a3, stats, down_own, down_other, grads = hidden_layer(
        info, tokens, cot, merged, wt, weights, groups
    )
    r1 = send(a1, routes[1])
    r3 = send(a3, routes[3])
    r2 = send(a2, routes[2])
    if split == 1:
        grads = grads[0].reshape(groups + 1, dp, share, model).transpose(1, 0, 2, 3)
        grads = grads.reshape(dp, (groups + 1) * share, model)
        down_pieces = [
            lax.psum_scatter(
                down_own.reshape(dp, -1, model), "dp", scatter_dimension=0, tiled=True
            )[0]
        ]
    else:
        down_got = send(down_other, other_core)
        chip = row >> 1

        def down_piece(j):
            mine_at = [
                lax.dynamic_index_in_dim(v, chip ^ j, 0, keepdims=False).astype(F32)
                for v in (down_own, down_got)
            ]
            return (mine_at[0] + mine_at[1]).astype(BF)

        down_pieces = [down_piece(0)]
        down_pieces += [send(down_piece(j), flipped(j << 1)) for j in range(1, dp // 2)]
    reduced = lax.psum_scatter(grads, "dp", scatter_dimension=0, tiled=True)[0]

    layer_out, r3 = together(layer_out, r3)
    layer_moved = send(layer_out, swap)
    def to_owner(value, owner):
        return send(value, lambda d, z: None if (d & 1) == owner else (d ^ 1, z))

    def to_chip(value, owner):
        return send(value, lambda d, z: (d, z ^ 1) if (d & 1) == owner else None)

    def home_from(owner):
        return lambda d, z: None if at_home(d, z) or (d & 1) != owner else (d ^ 1, z ^ 2)

    all_grads = [a0, r1, r2, r3]
    near, far, stacked, *state = attend_backward(info, packed, outs, all_grads, logsum, wt)
    near, far, layer_moved, *down_pieces = together(near, far, layer_moved, *down_pieces)
    down_sum = sum([p.astype(F32) for p in down_pieces[1:]], down_pieces[0].astype(F32))
    down_sum = down_sum.astype(BF)
    far_other, near_other = to_owner(far, 1), to_owner(near, 1)
    partial = (far.astype(F32) + far_other.astype(F32)).astype(BF)
    partial, stacked = together(partial, stacked)
    far_chip = to_chip(partial, 1)
    dw = project_grad(stacked, normed, 1)
    state[0], dw, reduced = together(state[0], dw, reduced)
    reduced = jnp.concatenate([down_sum, reduced])
    scattered = lax.psum_scatter(reduced, "seq", scatter_dimension=0, tiled=True)
    near_b, far_b, stacked = attend_backward(
        info, packed, outs, all_grads, logsum, wt, state
    )
    far_chip, far_b, near_b = together(far_chip, far_b, near_b)
    far_b_other, near_b_other = to_owner(far_b, 0), to_owner(near_b, 0)
    far_b_other, scattered = together(far_b_other, scattered)
    partial = (far_b.astype(F32) + far_b_other.astype(F32)).astype(BF)
    partial, stacked, far_chip = together(partial, stacked, far_chip)
    far_b_chip = to_chip(partial, 0)
    input_grad, low_a, stats = final_norm(
        1, info, tokens, [near, near_other, far_chip], resid_grad, wt, stats
    )
    dw = project_grad(stacked, normed, 0, dw)
    far_b_chip, scattered, low_a, dw = together(far_b_chip, scattered, low_a, dw)
    moved_a = send(low_a, home_from(1))
    total = lax.all_gather(scattered, "seq", axis=0, tiled=True)
    input_grad, low_b, stats = final_norm(
        0, info, tokens, [near_b, near_b_other, far_b_chip], resid_grad, wt, stats, input_grad
    )
    moved_b = send(low_b, home_from(0))

    small = jnp.pad(stats.T, ((0, 0), (0, 56))).astype(BF)
    current = jnp.concatenate([dw, small], axis=1).reshape(dp, share, 3 * width + 64)
    top = bits - 1
    while top > 0:
        width_bits = 2 if top > 1 else 1
        quarter = current.shape[0] >> width_bits
        low_bit = top - width_bits + 1
        mine_at = (row >> low_bit) & ((1 << width_bits) - 1)

        def piece(j):
            return lax.dynamic_slice_in_dim(current, (mine_at ^ j) * quarter, quarter, 0)

        pieces = [piece(0)]
        pieces += [send(piece(j), flipped(j << low_bit)) for j in range(1, 1 << width_bits)]
        moved_a, *pieces = together(moved_a, *pieces)
        summed = sum([p.astype(F32) for p in pieces[1:]], pieces[0].astype(F32))
        current = summed.astype(BF)
        top -= width_bits
    got = send(current, lambda d, z: (d, z ^ 2))
    got, moved_b, total = together(got, moved_b, total)
    input_moved = jnp.where(core == 0, moved_a, moved_b)
    current = (current.astype(F32) + got.astype(F32)).astype(BF)
    upper = core == 1
    give = jnp.where(upper, current[0], current[1])
    keep = jnp.where(upper, current[1], current[0])
    got = send(give, other_core)
    pair = jnp.where(upper, jnp.stack([got, keep]), jnp.stack([keep, got]))
    far = send(pair, next_chip)
    odd = (line & 1) == 1
    quad = [
        jnp.where(odd, far[0], pair[0]),
        jnp.where(odd, pair[0], far[0]),
        jnp.where(odd, far[1], pair[1]),
        jnp.where(odd, pair[1], far[1]),
    ]
    proj_grad = jnp.concatenate(
        [q[:, p * width : (p + 1) * width] for p in range(3) for q in quad], axis=1
    ).astype(F32)
    small = sum([q[:, 3 * width :].astype(F32) for q in quad[1:]], quad[0][:, 3 * width :].astype(F32))
    small = small.T
    total = total.astype(F32)

    tall = hidden_down.shape[0]
    down_grad = total[:tall]
    up_grad = jnp.concatenate(
        [total[tall + k * share : tall + (k + 1) * share] for k in range(groups)], axis=1
    )
    out_grad = total[tall + groups * share :]
    return (
        jnp.where(stays, layer_out, layer_moved)[None],
        jnp.where(stays, input_grad, input_moved.astype(F32))[None],
        small[4],
        small[2],
        small[3],
        proj_grad,
        out_grad,
        small[0],
        small[1],
        up_grad,
        down_grad,
    )


def solution(mesh):
    vector, matrix, tokens = P("dp"), P("dp", None), P("dp", "seq", None)
    return jax.shard_map(
        functools.partial(on_device, mesh.shape["dp"]),
        mesh=mesh,
        in_specs=(
            tokens,
            vector,
            vector,
            vector,
            matrix,
            matrix,
            vector,
            vector,
            matrix,
            matrix,
            tokens,
        ),
        out_specs=(
            tokens,
            tokens,
            vector,
            vector,
            vector,
            matrix,
            matrix,
            vector,
            vector,
            matrix,
            matrix,
        ),
        check_vma=False,
    )
```

profile of v0, /device:TPU:0, one launch (start us, length us, event | category | flops | bytes accessed | tf_op | source)
XLA Modules:
  0.0 378.8 jit_solution(16581420618532357580)
XLA Ops:
  10.2 3.0 collective-permute-start
  13.2 1.6 reshape.60
  19.2 1.6 collective-permute-start.4
  20.8 1.5 collective-permute-start.2
  22.8 9.5 %collective-permute-done.4 = bf16[2,96,640]{2,1,0:T(8,128)(2,1)S(1)} collective-permute-done((bf16[2,96,640]{2,1,0:T(8,128)(2,1)S(1)}, bf16[2,96,640]{2,1,0:T(8,128)(2,1)S(1)}, u32[]{:S(2)}, u32[]{:S(2)}) %collective-permute-start.4) | collective-permute-done | bytes 245792 | tf_op jit(solution)/shard_map/ppermute | solution.py:722
  32.4 10.6 %collective-permute-done.2 = bf16[2,96,640]{2,1,0:T(8,128)(2,1)S(1)} collective-permute-done((bf16[2,96,640]{2,1,0:T(8,128)(2,1)S(1)}, bf16[2,96,640]{2,1,0:T(8,128)(2,1)S(1)}, u32[]{:S(2)}, u32[]{:S(2)}) %collective-permute-start.2) | collective-permute-done | bytes 245792 | tf_op jit(solution)/shard_map/ppermute | solution.py:722
  44.3 1.7 collective-permute-start.5
  46.6 2.3 copy.44
  49.9 11.3 %norm_project.2 = (bf16[576,3072]{1,0:T(8,128)(2,1)}, bf16[3072,768]{1,0:T(8,128)(2,1)}) custom-call(s32[4]{0:T(128)} %pad_add_fusion.2.info, bf16[768,768]{1,0:T(8,128)(2,1)} %bitcast.61, bf16[768,768]{1,0:T(8,128)(2,1)} %collective-permute-done.6.refs_1_, bf16[768,768]{1,0:T(8,128)(2,1)} %copy-done, bf16[768,768]{1,0:T(8,128)(2,1)} %copy-done.5, ...), custom_call_target="tpu_custom_call" | custom-call | flops 2038431744 | bytes 10616832 | tf_op jit(solution)/shard_map/norm_project/pallas_call | solution.py:95
  61.2 3.7 collective-permute-start.8
  68.6 5.2 %norm_project.3 = (bf16[576,3072]{1,0:T(8,128)(2,1)}, bf16[3072,768]{1,0:T(8,128)(2,1)}) custom-call(s32[2]{0:T(128)} %pad_add_fusion.1.info, bf16[768,768]{1,0:T(8,128)(2,1)} %copy-done.14, bf16[768,768]{1,0:T(8,128)(2,1)} %collective-permute-done.5.refs_1_, bf16[640,768]{1,0:T(8,128)(2,1)} %bitcast.55, ...), custom_call_target="tpu_custom_call", output_to_operand_aliasing={{0}: (4, {}), {1}: (5, {})} | custom-call | flops 679477248 | bytes 3538944 | tf_op jit(solution)/shard_map/norm_project/pallas_call | solution.py:95
  73.9 28.5 %attention_forward.1 = (bf16[192,768]{1,0:T(8,128)(2,1)}, bf16[192,768]{1,0:T(8,128)(2,1)}, bf16[192,768]{1,0:T(8,128)(2,1)}, bf16[192,768]{1,0:T(8,128)(2,1)}, f32[8,3072]{1,0:T(8,128)}) custom-call(s32[3]{0:T(128)} %pad_add_fusion.info, bf16[576,3072]{1,0:T(8,128)(2,1)} %get-tuple-element.92.packed), custom_call_target="tpu_custom_call" | custom-call | flops 589824 | bytes 589824 | tf_op jit(solution)/shard_map/attention_forward/pallas_call | solution.py:203
  103.1 1.4 collective-permute-start.12
  106.8 5.7 %collective-permute-done.10.m1 = bf16[192,768]{1,0:T(8,128)(2,1)} collective-permute-done((bf16[192,768]{1,0:T(8,128)(2,1)}, bf16[192,768]{1,0:T(8,128)(2,1)}, u32[]{:S(2)}, u32[]{:S(2)}) %collective-permute-start.10) | collective-permute-done | bytes 294944 | tf_op jit(solution)/shard_map/ppermute | solution.py:722
  112.6 5.7 %collective-permute-done.12.m3 = bf16[192,768]{1,0:T(8,128)(2,1)} collective-permute-done((bf16[192,768]{1,0:T(8,128)(2,1)}, bf16[192,768]{1,0:T(8,128)(2,1)}, u32[]{:S(2)}, u32[]{:S(2)}) %collective-permute-start.12) | collective-permute-done | bytes 294944 | tf_op jit(solution)/shard_map/ppermute | solution.py:722
  118.2 39.0 %hidden_layer.1 = (bf16[768,768]{1,0:T(8,128)(2,1)}, f32[768,768]{1,0:T(8,128)}, bf16[192,768]{1,0:T(8,128)(2,1)}, bf16[192,768]{1,0:T(8,128)(2,1)}, bf16[192,76...) custom-call(s32[3]{0:T(128)} %pad_add_fusion.info, ...), custom_call_target="tpu_custom_call" | custom-call | flops 24461180928 | bytes 28311552 | tf_op jit(solution)/shard_map/hidden_layer/pallas_call | solution.py:581
  158.0 1.5 collective-permute-start.14
  159.5 7.0 %collective-permute-done.13.g3 = bf16[192,768]{1,0:T(8,128)(2,1)S(1)} collective-permute-done((bf16[192,768]{1,0:T(8,128)(2,1)}, bf16[192,768]{1,0:T(8,128)(2,1)S(1)}, u32[]{:S(2)}, u32[]{:S(2)}) %collective-permute-start.13) | collective-permute-done | bytes 294944 | tf_op jit(solution)/shard_map/ppermute | solution.py:722
  166.5 1.7 collective-permute-start.16
  168.2 3.7 fusion.5
  171.9 1.8 collective-permute-start.18
  173.7 1.4 collective-permute-start.19
  176.7 43.1 %attention_backward.2 = (bf16[768,768]{1,0:T(8,128)(2,1)}, bf16[768,768]{1,0:T(8,128)(2,1)}, bf16[576,1536]{1,0:T(8,128)(2,1)}, f32[3,1536,64]{2,1,0:T(8,128)}, f32[3,1536,64]{2,1,0:T(8,128)}) custom-call(s32[3]{0:T(128)} %pad_add_fusion.info, bf16[576,3072]{1,0:T(8,128)(2,1)} %get-tuple-element.92.packed, bf16[192,768]{1,0:T(8,128)(2,1)} %get-tuple-element.97.m0.o0, ...), custom_call_target="tpu_custom_call" | custom-call | flops 158544691200 | bytes 11796480 | tf_op jit(solution)/shard_map/attention_backward/pallas_call | solution.py:351
  219.9 2.1 collective-permute-start.21
  222.0 1.9 add_convert_fusion.2
  226.4 4.7 %project_grad.2.refs_2_ = f32[576,768]{1,0:T(8,128)} custom-call(bf16[576,1536]{1,0:T(8,128)(2,1)} %get-tuple-element.118.refs_0_, bf16[3072,768]{1,0:T(8,128)(2,1)} %get-tuple-element.119.refs_1_), custom_call_target="tpu_custom_call" | custom-call | flops 1358954496 | bytes 4128768 | tf_op jit(solution)/shard_map/project_grad/pallas_call | solution.py:405
  231.2 2.6 reduce-scatter.3.cloned.1.call-done
  233.8 2.3 pad_maximum_fusion
  236.2 22.9 %attention_backward.3 = (bf16[768,768]{1,0:T(8,128)(2,1)}, bf16[768,768]{1,0:T(8,128)(2,1)}, bf16[576,1536]{1,0:T(8,128)(2,1)}) custom-call(s32[3]{0:T(128)} %pad_add_fusion.info, bf16[576,3072]{1,0:T(8,128)(2,1)} %get-tuple-element.92.packed, bf16[192,768]{1,0:T(8,128)(2,1)} %get-tuple-element.97.m0.o0, bf16[192,768]{1,0:T(8,128)(2,1)} %get-tuple-element.98.o1, ...), custom_call_target="tpu_custom_call" | custom-call | flops 67947724800 | bytes 11796480 | tf_op jit(solution)/shard_map/attention_backward/pallas_call | solution.py:351
  260.4 5.1 %collective-permute-start.26 = (bf16[768,768]{1,0:T(8,128)(2,1)S(1)}, bf16[768,768]{1,0:T(8,128)(2,1)}, u32[]{:S(2)}, u32[]{:S(2)}) collective-permute-start(bf16[768,768]{1,0:T(8,128)(2,1)S(1)} %copy-done.12), channel_id=1, source_target_pairs={{0,4},{1,5},{2,6},{3,7},{8,12},{9,13},{10,14},{11,15},{16,20},{17,... | collective-permute-start | bytes 3538952 | tf_op jit(solution)/shard_map/ppermute | solution.py:722
  265.6 2.5 reduce-scatter.5.cloned.1.call-done
  268.1 2.0 add_convert_fusion
  270.1 1.9 collective-permute-start.25
  272.1 1.5 collective-permute-start.23
  273.6 5.1 %final_norm.2 = (f32[768,768]{1,0:T(8,128)}, bf16[768,768]{1,0:T(8,128)(2,1)}, f32[8,768]{1,0:T(8,128)}) custom-call(s32[3]{0:T(128)} %pad_add_fusion.info, bf16[768,768]{1,0:T(8,128)(2,1)} %broadcast_select_fusion.1.tok, bf16[768,768]{1,0:T(8,128)(2,1)} %get-tuple-element.137.p0, bf16[768,768]{1,0:T(8,128)(2,1)} %collective-permute-done.26.p1, ...), custom_call_target="tpu_custom_call" | custom-call | flops 589824 | bytes 589824 | tf_op jit(solution)/shard_map/final_norm/pallas_call | solution.py:662
  278.7 5.3 %project_grad.3 = bf16[768,576]{1,0:T(8,128)(2,1)} custom-call(bf16[576,1536]{1,0:T(8,128)(2,1)} %get-tuple-element.142.refs_0_, bf16[3072,768]{1,0:T(8,128)(2,1)} %get-tuple-element.119.refs_1_, f32[576,768]{1,0:T(8,128)} %project_grad.2.refs_2_), custom_call_target="tpu_custom_call" | custom-call | flops 1358954496 | bytes 4128768 | tf_op jit(solution)/shard_map/project_grad/pallas_call | solution.py:405
  284.0 4.3 %collective-permute-done.25.p2 = bf16[768,768]{1,0:T(8,128)(2,1)} collective-permute-done((bf16[768,768]{1,0:T(8,128)(2,1)S(1)}, bf16[768,768]{1,0:T(8,128)(2,1)}, u32[]{:S(2)}, u32[]{:S(2)}) %collective-permute-start.25) | collective-permute-done | bytes 1179680 | tf_op jit(solution)/shard_map/ppermute | solution.py:722
  289.1 7.0 %final_norm.3 = (f32[768,768]{1,0:T(8,128)}, bf16[768,768]{1,0:T(8,128)(2,1)}, f32[8,768]{1,0:T(8,128)}) custom-call(s32[3]{0:T(128)} %pad_add_fusion.info, bf16[768,768]{1,0:T(8,128)(2,1)} %broadcast_select_fusion.1.tok, bf16[768,768]{1,0:T(8,128)(2,1)} %get-tuple-element.125.p0, bf16[768,768]{1,0:T(8,128)(2,1)} %collective-permute-done.23.p1, ...), custom_call_target="tpu_custom_call" | custom-call | flops 589824 | bytes 589824 | tf_op jit(solution)/shard_map/final_norm/pallas_call | solution.py:662
  296.1 1.7 collective-permute-start.32
  299.0 1.5 collective-permute-start.28
  300.5 1.5 collective-permute-start.29
  302.5 4.5 %collective-permute-done.28 = bf16[2,96,640]{2,1,0:T(8,128)(2,1)S(1)} collective-permute-done((bf16[2,96,640]{2,1,0:T(8,128)(2,1)S(1)}, bf16[2,96,640]{2,1,0:T(8,128)(2,1)S(1)}, u32[]{:S(2)}, u32[]{:S(2)}) %collective-permute-start.28) | collective-permute-done | bytes 245792 | tf_op jit(solution)/shard_map/ppermute | solution.py:722
  307.1 7.1 %collective-permute-done.29 = bf16[2,96,640]{2,1,0:T(8,128)(2,1)S(1)} collective-permute-done((bf16[2,96,640]{2,1,0:T(8,128)(2,1)S(1)}, bf16[2,96,640]{2,1,0:T(8,128)(2,1)S(1)}, u32[]{:S(2)}, u32[]{:S(2)}) %collective-permute-start.29) | collective-permute-done | bytes 245792 | tf_op jit(solution)/shard_map/ppermute | solution.py:722
  314.3 12.0 %collective-permute-start.31 = (bf16[2,96,640]{2,1,0:T(8,128)(2,1)S(1)}, bf16[2,96,640]{2,1,0:T(8,128)(2,1)}, u32[]{:S(2)}, u32[]{:S(2)}) collective-permute-start(bf16[2,96,640]{2,1,0:T(8,128)(2,1)S(1)} %add_convert_fusion.8), channel_id=1, source_target_pairs={{0,2},{1,3},{2,0},{3,1},{4,6},{5,7},{6,4},{7,5},{8,10},{9,11},{10,... | collective-permute-start | bytes 737288 | tf_op jit(solution)/shard_map/ppermute | solution.py:722
  326.3 2.6 select_bitcast_fusion.1
  328.8 27.6 %collective-permute-done.31 = bf16[2,96,640]{2,1,0:T(8,128)(2,1)} collective-permute-done((bf16[2,96,640]{2,1,0:T(8,128)(2,1)S(1)}, bf16[2,96,640]{2,1,0:T(8,128)(2,1)}, u32[]{:S(2)}, u32[]{:S(2)}) %collective-permute-start.31) | collective-permute-done | bytes 245792 | tf_op jit(solution)/shard_map/ppermute | solution.py:722
  357.7 1.7 select_bitcast_fusion
  362.6 6.8 %collective-permute-done.34 = bf16[2,96,640]{2,1,0:T(8,128)(2,1)S(1)} collective-permute-done((bf16[2,96,640]{2,1,0:T(8,128)(2,1)S(1)}, bf16[2,96,640]{2,1,0:T(8,128)(2,1)S(1)}, u32[]{:S(2)}, u32[]{:S(2)}) %collective-permute-start.34) | collective-permute-done | bytes 245792 | tf_op jit(solution)/shard_map/ppermute | solution.py:722
  (147 shorter events, 32.9 us)
Async XLA Ops:
  7.2 111.0 %all-gather.6.cloned.1.call-start = ((), (), s32[]{:S(2)}) async-start(), calls=%async_computation.5 | async-start | bytes 11943936 | tf_op jit(solution)/shard_map/all_gather | solution.py:788
  9.6 224.2 %reduce-scatter.3.cloned.1.call-start = ((), (), s32[]{:S(2)}) async-start(), calls=%async_computation.2 | async-start | bytes 6635520 | tf_op jit(solution)/shard_map/reduce_scatter | solution.py:844
  10.2 34.1 %collective-permute-start = (bf16[768,768]{1,0:T(8,128)(2,1)S(1)}, bf16[768,768]{1,0:T(8,128)(2,1)S(1)}, u32[]{:S(2)}, u32[]{:S(2)}) collective-permute-start(bf16[768,768]{1,0:T(8,128)(2,1)S(1)} %bitcast.62), channel_id=1, source_target_pairs={{0,1},{1,0},{2,4},{3,5},{4,2},{5,3},{6,7},{7,6},{8,9},{9,8},{10,12... | collective-permute-start | bytes 3538952 | tf_op jit(solution)/shard_map/ppermute | solution.py:722
  17.0 2.2 collective-permute-start.1
  19.2 13.1 %collective-permute-start.4 = (bf16[2,96,640]{2,1,0:T(8,128)(2,1)S(1)}, bf16[2,96,640]{2,1,0:T(8,128)(2,1)S(1)}, u32[]{:S(2)}, u32[]{:S(2)}) collective-permute-start(bf16[2,96,640]{2,1,0:T(8,128)(2,1)S(1)} %maximum_select_fusion.3), channel_id=1, source_target_pairs={{0,8},{1,9},{2,10},{3,11},{4,12},{5,13},{6,14},{7,15},{8,0},{9,1},... | collective-permute-start | bytes 737288 | tf_op jit(solution)/shard_map/ppermute | solution.py:722
  20.8 22.3 %collective-permute-start.2 = (bf16[2,96,640]{2,1,0:T(8,128)(2,1)S(1)}, bf16[2,96,640]{2,1,0:T(8,128)(2,1)S(1)}, u32[]{:S(2)}, u32[]{:S(2)}) collective-permute-start(bf16[2,96,640]{2,1,0:T(8,128)(2,1)S(1)} %maximum_select_fusion.3), channel_id=1, source_target_pairs={{0,24},{1,25},{2,26},{3,27},{4,28},{5,29},{6,30},{7,31},{8,16},{9,... | collective-permute-start | bytes 737288 | tf_op jit(solution)/shard_map/ppermute | solution.py:722
  22.3 20.8 %collective-permute-start.3 = (bf16[2,96,640]{2,1,0:T(8,128)(2,1)S(1)}, bf16[2,96,640]{2,1,0:T(8,128)(2,1)S(1)}, u32[]{:S(2)}, u32[]{:S(2)}) collective-permute-start(bf16[2,96,640]{2,1,0:T(8,128)(2,1)S(1)} %maximum_select_fusion.3), channel_id=1, source_target_pairs={{0,16},{1,17},{2,18},{3,19},{4,20},{5,21},{6,22},{7,23},{8,24},{9,... | collective-permute-start | bytes 737288 | tf_op jit(solution)/shard_map/ppermute | solution.py:722
  22.8 26.1 %collective-permute-start.6 = (bf16[768,768]{1,0:T(8,128)(2,1)S(1)}, bf16[768,768]{1,0:T(8,128)(2,1)}, u32[]{:S(2)}, u32[]{:S(2)}) collective-permute-start(bf16[768,768]{1,0:T(8,128)(2,1)S(1)} %bitcast.63), channel_id=1, source_target_pairs={{0,4},{1,5},{2,6},{3,7},{4,0},{5,1},{6,2},{7,3},{8,12},{9,13},{10,... | collective-permute-start | bytes 3538952 | tf_op jit(solution)/shard_map/ppermute | solution.py:722
  44.3 4.6 %collective-permute-start.7 = (bf16[768,768]{1,0:T(8,128)(2,1)S(1)}, bf16[768,768]{1,0:T(8,128)(2,1)S(1)}, u32[]{:S(2)}, u32[]{:S(2)}) collective-permute-start(bf16[768,768]{1,0:T(8,128)(2,1)S(1)} %collective-permute-done.refs_2_.refs_5_), channel_id=1, source_target_pairs={{0,4},{1,5},{2,6},{3,7},{4,0},{5,1},{6,2},{7,3},{8,12},{9,13},{10,... | collective-permute-start | bytes 3538952 | tf_op jit(solution)/shard_map/ppermute | solution.py:722
  44.3 16.9 %collective-permute-start.5 = (bf16[768,768]{1,0:T(8,128)(2,1)S(1)}, bf16[768,768]{1,0:T(8,128)(2,1)}, u32[]{:S(2)}, u32[]{:S(2)}) collective-permute-start(bf16[768,768]{1,0:T(8,128)(2,1)S(1)} %collective-permute-done.refs_2_.refs_5_), channel_id=1, source_target_pairs={{2,3},{3,2},{4,5},{5,4},{10,11},{11,10},{12,13},{13,12},{18,19},{1... | collective-permute-start | bytes 3538952 | tf_op jit(solution)/shard_map/ppermute | solution.py:722
  61.2 6.4 %collective-permute-start.8 = (bf16[768,768]{1,0:T(8,128)(2,1)}, bf16[768,768]{1,0:T(8,128)(2,1)S(1)}, u32[]{:S(2)}, u32[]{:S(2)}) collective-permute-start(bf16[768,768]{1,0:T(8,128)(2,1)} %collective-permute-done.5.refs_1_), channel_id=1, source_target_pairs={{0,4},{1,5},{2,6},{3,7},{4,0},{5,1},{6,2},{7,3},{8,12},{9,13},{10,... | collective-permute-start | bytes 3538952 | tf_op jit(solution)/shard_map/ppermute | solution.py:722
  64.9 40.7 %collective-permute-start.9 = (bf16[768,768]{1,0:T(8,128)(2,1)}, bf16[768,768]{1,0:T(8,128)(2,1)S(1)}, u32[]{:S(2)}, u32[]{:S(2)}) collective-permute-start(bf16[768,768]{1,0:T(8,128)(2,1)} %bitcast.68), channel_id=1, source_target_pairs={{2,4},{3,5},{4,2},{5,3},{10,12},{11,13},{12,10},{13,11},{18,20},{1... | collective-permute-start | bytes 3538952 | tf_op jit(solution)/shard_map/ppermute | solution.py:722
  73.9 30.7 %copy-start.1 = (bf16[768,768]{1,0:T(8,128)(2,1)S(1)}, bf16[768,768]{1,0:T(8,128)(2,1)}, u32[]{:S(2)}) copy-start(bf16[768,768]{1,0:T(8,128)(2,1)} %copy-done) | copy-start | bytes 3538948
  73.9 30.7 %copy-start.4 = (bf16[1,768,768]{2,1,0:T(8,128)(2,1)S(1)}, bf16[1,768,768]{2,1,0:T(8,128)(2,1)}, u32[]{:S(2)}) copy-start(bf16[1,768,768]{2,1,0:T(8,128)(2,1)} %param.11) | copy-start | bytes 3538948
  102.4 10.2 %collective-permute-start.10 = (bf16[192,768]{1,0:T(8,128)(2,1)}, bf16[192,768]{1,0:T(8,128)(2,1)}, u32[]{:S(2)}, u32[]{:S(2)}) collective-permute-start(bf16[192,768]{1,0:T(8,128)(2,1)} %get-tuple-element.98.o1), channel_id=1, source_target_pairs={{0,1},{1,0},{2,3},{3,2},{4,5},{5,4},{6,7},{7,6},{8,9},{9,8},{10,11... | collective-permute-start | bytes 884744 | tf_op jit(solution)/shard_map/ppermute | solution.py:722
  102.4 10.2 %collective-permute-start.11 = (bf16[192,768]{1,0:T(8,128)(2,1)}, bf16[192,768]{1,0:T(8,128)(2,1)}, u32[]{:S(2)}, u32[]{:S(2)}) collective-permute-start(bf16[192,768]{1,0:T(8,128)(2,1)} %get-tuple-element.99.o2), channel_id=1, source_target_pairs={{0,4},{1,5},{2,6},{3,7},{4,0},{5,1},{6,2},{7,3},{8,12},{9,13},{10,... | collective-permute-start | bytes 884744 | tf_op jit(solution)/shard_map/ppermute | solution.py:722
  103.1 15.1 %collective-permute-start.12 = (bf16[192,768]{1,0:T(8,128)(2,1)}, bf16[192,768]{1,0:T(8,128)(2,1)}, u32[]{:S(2)}, u32[]{:S(2)}) collective-permute-start(bf16[192,768]{1,0:T(8,128)(2,1)} %get-tuple-element.100.o3), channel_id=1, source_target_pairs={{0,5},{1,4},{2,7},{3,6},{4,1},{5,0},{6,3},{7,2},{8,13},{9,12},{10,... | collective-permute-start | bytes 884744 | tf_op jit(solution)/shard_map/ppermute | solution.py:722
  157.3 11.0 %collective-permute-start.17 = (bf16[4,384,768]{2,1,0:T(8,128)(2,1)}, bf16[4,384,768]{2,1,0:T(8,128)(2,1)}, u32[]{:S(2)}, u32[]{:S(2)}) collective-permute-start(bf16[4,384,768]{2,1,0:T(8,128)(2,1)} %get-tuple-element.112), channel_id=1, source_target_pairs={{0,4},{1,5},{2,6},{3,7},{4,0},{5,1},{6,2},{7,3},{8,12},{9,13},{10,... | collective-permute-start | bytes 7077896 | tf_op jit(solution)/shard_map/ppermute | solution.py:722
  157.5 9.1 %collective-permute-start.13 = (bf16[192,768]{1,0:T(8,128)(2,1)}, bf16[192,768]{1,0:T(8,128)(2,1)S(1)}, u32[]{:S(2)}, u32[]{:S(2)}) collective-permute-start(bf16[192,768]{1,0:T(8,128)(2,1)} %get-tuple-element.102), channel_id=1, source_target_pairs={{0,5},{1,4},{2,7},{3,6},{4,1},{5,0},{6,3},{7,2},{8,13},{9,12},{10,... | collective-permute-start | bytes 884744 | tf_op jit(solution)/shard_map/ppermute | solution.py:722
  158.0 17.1 %collective-permute-start.14 = (bf16[192,768]{1,0:T(8,128)(2,1)}, bf16[192,768]{1,0:T(8,128)(2,1)S(1)}, u32[]{:S(2)}, u32[]{:S(2)}) collective-permute-start(bf16[192,768]{1,0:T(8,128)(2,1)} %get-tuple-element.105), channel_id=1, source_target_pairs={{0,1},{1,0},{2,3},{3,2},{4,5},{5,4},{6,7},{7,6},{8,9},{9,8},{10,11... | collective-permute-start | bytes 884744 | tf_op jit(solution)/shard_map/ppermute | solution.py:722
  159.5 16.5 %collective-permute-start.15 = (bf16[192,768]{1,0:T(8,128)(2,1)}, bf16[192,768]{1,0:T(8,128)(2,1)S(1)}, u32[]{:S(2)}, u32[]{:S(2)}) collective-permute-start(bf16[192,768]{1,0:T(8,128)(2,1)} %get-tuple-element.106), channel_id=1, source_target_pairs={{0,4},{1,5},{2,6},{3,7},{4,0},{5,1},{6,2},{7,3},{8,12},{9,13},{10,... | collective-permute-start | bytes 884744 | tf_op jit(solution)/shard_map/ppermute | solution.py:722
  159.5 8.8 %copy-start.9 = (bf16[4,384,768]{2,1,0:T(8,128)(2,1)S(1)}, bf16[4,384,768]{2,1,0:T(8,128)(2,1)}, u32[]{:S(2)}) copy-start(bf16[4,384,768]{2,1,0:T(8,128)(2,1)} %get-tuple-element.111) | copy-start | bytes 7077892
  159.5 108.6 %reduce-scatter.5.cloned.1.call-start = ((), (), s32[]{:S(2)}) async-start(), calls=%async_computation.3 | async-start | bytes 1658880 | tf_op jit(solution)/shard_map/reduce_scatter | solution.py:869
  166.5 53.4 %collective-permute-start.16 = (bf16[768,768]{1,0:T(8,128)(2,1)}, bf16[768,768]{1,0:T(8,128)(2,1)}, u32[]{:S(2)}, u32[]{:S(2)}) collective-permute-start(bf16[768,768]{1,0:T(8,128)(2,1)} %get-tuple-element.103), channel_id=1, source_target_pairs={{2,4},{3,5},{4,2},{5,3},{10,12},{11,13},{12,10},{13,11},{18,20},{1... | collective-permute-start | bytes 3538952 | tf_op jit(solution)/shard_map/ppermute | solution.py:722
  171.9 48.0 %collective-permute-start.18 = (bf16[384,768]{1,0:T(8,128)(2,1)}, bf16[384,768]{1,0:T(8,128)(2,1)}, u32[]{:S(2)}, u32[]{:S(2)}) collective-permute-start(bf16[384,768]{1,0:T(8,128)(2,1)} %get-tuple-element.168), channel_id=1, source_target_pairs={{0,8},{1,9},{2,10},{3,11},{4,12},{5,13},{6,14},{7,15},{8,0},{9,1},... | collective-permute-start | bytes 1769480 | tf_op jit(solution)/shard_map/ppermute | solution.py:722
  173.7 46.2 %collective-permute-start.19 = (bf16[384,768]{1,0:T(8,128)(2,1)}, bf16[384,768]{1,0:T(8,128)(2,1)}, u32[]{:S(2)}, u32[]{:S(2)}) collective-permute-start(bf16[384,768]{1,0:T(8,128)(2,1)} %get-tuple-element.167), channel_id=1, source_target_pairs={{0,16},{1,17},{2,18},{3,19},{4,20},{5,21},{6,22},{7,23},{8,24},{9,... | collective-permute-start | bytes 1769480 | tf_op jit(solution)/shard_map/ppermute | solution.py:722
  175.1 44.8 %collective-permute-start.20 = (bf16[384,768]{1,0:T(8,128)(2,1)}, bf16[384,768]{1,0:T(8,128)(2,1)}, u32[]{:S(2)}, u32[]{:S(2)}) collective-permute-start(bf16[384,768]{1,0:T(8,128)(2,1)} %get-tuple-element.166), channel_id=1, source_target_pairs={{0,24},{1,25},{2,26},{3,27},{4,28},{5,29},{6,30},{7,31},{8,16},{9,... | collective-permute-start | bytes 1769480 | tf_op jit(solution)/shard_map/ppermute | solution.py:722
  176.7 45.3 %copy-start.10 = (bf16[384,768]{1,0:T(8,128)(2,1)S(1)}, bf16[384,768]{1,0:T(8,128)(2,1)}, u32[]{:S(2)}) copy-start(bf16[384,768]{1,0:T(8,128)(2,1)} %get-tuple-element.127) | copy-start | bytes 1769476
  219.9 4.4 %collective-permute-start.21 = (bf16[768,768]{1,0:T(8,128)(2,1)}, bf16[768,768]{1,0:T(8,128)(2,1)S(1)}, u32[]{:S(2)}, u32[]{:S(2)}) collective-permute-start(bf16[768,768]{1,0:T(8,128)(2,1)} %get-tuple-element.114), channel_id=1, source_target_pairs={{0,4},{1,5},{2,6},{3,7},{8,12},{9,13},{10,14},{11,15},{16,20},{17,... | collective-permute-start | bytes 3538952 | tf_op jit(solution)/shard_map/ppermute | solution.py:722
  225.7 33.4 %collective-permute-start.22 = (bf16[768,768]{1,0:T(8,128)(2,1)}, bf16[768,768]{1,0:T(8,128)(2,1)S(1)}, u32[]{:S(2)}, u32[]{:S(2)}) collective-permute-start(bf16[768,768]{1,0:T(8,128)(2,1)} %add_convert_fusion.1), channel_id=1, source_target_pairs={{4,5},{5,4},{6,7},{7,6},{12,13},{13,12},{14,15},{15,14},{20,21},{2... | collective-permute-start | bytes 3538952 | tf_op jit(solution)/shard_map/ppermute | solution.py:722
  236.1 120.4 %all-gather.4.cloned.1.call-start = ((), (), s32[]{:S(2)}) async-start(), calls=%async_computation.4 | async-start | bytes 1658880 | tf_op jit(solution)/shard_map/all_gather | solution.py:885
  236.2 24.3 %copy-start.12 = (bf16[768,768]{1,0:T(8,128)(2,1)S(1)}, bf16[768,768]{1,0:T(8,128)(2,1)}, u32[]{:S(2)}) copy-start(bf16[768,768]{1,0:T(8,128)(2,1)} %get-tuple-element.137.p0) | copy-start | bytes 3538948
  259.1 9.0 %copy-start.13 = (bf16[768,768]{1,0:T(8,128)(2,1)}, bf16[768,768]{1,0:T(8,128)(2,1)S(1)}, u32[]{:S(2)}) copy-start(bf16[768,768]{1,0:T(8,128)(2,1)S(1)} %collective-permute-done.22.p2) | copy-start | bytes 3538948
  259.1 6.5 %collective-permute-start.24 = (bf16[768,768]{1,0:T(8,128)(2,1)}, bf16[768,768]{1,0:T(8,128)(2,1)}, u32[]{:S(2)}, u32[]{:S(2)}) collective-permute-start(bf16[768,768]{1,0:T(8,128)(2,1)} %get-tuple-element.126), channel_id=1, source_target_pairs={{4,0},{5,1},{6,2},{7,3},{12,8},{13,9},{14,10},{15,11},{20,16},{21,... | collective-permute-start | bytes 3538952 | tf_op jit(solution)/shard_map/ppermute | solution.py:722
  260.4 13.2 %collective-permute-start.26 = (bf16[768,768]{1,0:T(8,128)(2,1)S(1)}, bf16[768,768]{1,0:T(8,128)(2,1)}, u32[]{:S(2)}, u32[]{:S(2)}) collective-permute-start(bf16[768,768]{1,0:T(8,128)(2,1)S(1)} %copy-done.12), channel_id=1, source_target_pairs={{0,4},{1,5},{2,6},{3,7},{8,12},{9,13},{10,14},{11,15},{16,20},{17,... | collective-permute-start | bytes 3538952 | tf_op jit(solution)/shard_map/ppermute | solution.py:722
  270.1 18.2 %collective-permute-start.25 = (bf16[768,768]{1,0:T(8,128)(2,1)S(1)}, bf16[768,768]{1,0:T(8,128)(2,1)}, u32[]{:S(2)}, u32[]{:S(2)}) collective-permute-start(bf16[768,768]{1,0:T(8,128)(2,1)S(1)} %add_convert_fusion), channel_id=1, source_target_pairs={{0,1},{1,0},{2,3},{3,2},{8,9},{9,8},{10,11},{11,10},{16,17},{17,16... | collective-permute-start | bytes 3538952 | tf_op jit(solution)/shard_map/ppermute | solution.py:722
  272.1 17.1 %collective-permute-start.23 = (bf16[768,768]{1,0:T(8,128)(2,1)S(1)}, bf16[768,768]{1,0:T(8,128)(2,1)}, u32[]{:S(2)}, u32[]{:S(2)}) collective-permute-start(bf16[768,768]{1,0:T(8,128)(2,1)S(1)} %copy-done.11), channel_id=1, source_target_pairs={{4,0},{5,1},{6,2},{7,3},{12,8},{13,9},{14,10},{15,11},{20,16},{21,... | collective-permute-start | bytes 3538952 | tf_op jit(solution)/shard_map/ppermute | solution.py:722
  288.3 25.8 %collective-permute-start.27 = (bf16[768,768]{1,0:T(8,128)(2,1)}, bf16[768,768]{1,0:T(8,128)(2,1)S(1)}, u32[]{:S(2)}, u32[]{:S(2)}) collective-permute-start(bf16[768,768]{1,0:T(8,128)(2,1)} %get-tuple-element.148), channel_id=1, source_target_pairs={{4,2},{5,3},{12,10},{13,11},{20,18},{21,19},{28,26},{29,27}} | collective-permute-start | bytes 3538952 | tf_op jit(solution)/shard_map/ppermute | solution.py:722
  289.1 9.6 %copy-start.6 = (bf16[768,576]{1,0:T(8,128)(2,1)S(1)}, bf16[768,576]{1,0:T(8,128)(2,1)}, u32[]{:S(2)}) copy-start(bf16[768,576]{1,0:T(8,128)(2,1)} %project_grad.3) | copy-start | bytes 2654212
  296.1 32.8 %collective-permute-start.32 = (bf16[768,768]{1,0:T(8,128)(2,1)}, bf16[768,768]{1,0:T(8,128)(2,1)}, u32[]{:S(2)}, u32[]{:S(2)}) collective-permute-start(bf16[768,768]{1,0:T(8,128)(2,1)} %get-tuple-element.156), channel_id=1, source_target_pairs={{2,4},{3,5},{10,12},{11,13},{18,20},{19,21},{26,28},{27,29}} | collective-permute-start | bytes 3538952 | tf_op jit(solution)/shard_map/ppermute | solution.py:722
  299.0 8.1 %collective-permute-start.28 = (bf16[2,96,640]{2,1,0:T(8,128)(2,1)S(1)}, bf16[2,96,640]{2,1,0:T(8,128)(2,1)S(1)}, u32[]{:S(2)}, u32[]{:S(2)}) collective-permute-start(bf16[2,96,640]{2,1,0:T(8,128)(2,1)S(1)} %get-tuple-element.177), channel_id=1, source_target_pairs={{0,8},{1,9},{2,10},{3,11},{4,12},{5,13},{6,14},{7,15},{8,0},{9,1},... | collective-permute-start | bytes 737288 | tf_op jit(solution)/shard_map/ppermute | solution.py:722
  300.5 13.7 %collective-permute-start.29 = (bf16[2,96,640]{2,1,0:T(8,128)(2,1)S(1)}, bf16[2,96,640]{2,1,0:T(8,128)(2,1)S(1)}, u32[]{:S(2)}, u32[]{:S(2)}) collective-permute-start(bf16[2,96,640]{2,1,0:T(8,128)(2,1)S(1)} %get-tuple-element.176), channel_id=1, source_target_pairs={{0,16},{1,17},{2,18},{3,19},{4,20},{5,21},{6,22},{7,23},{8,24},{9,... | collective-permute-start | bytes 737288 | tf_op jit(solution)/shard_map/ppermute | solution.py:722
  302.0 12.2 %collective-permute-start.30 = (bf16[2,96,640]{2,1,0:T(8,128)(2,1)S(1)}, bf16[2,96,640]{2,1,0:T(8,128)(2,1)S(1)}, u32[]{:S(2)}, u32[]{:S(2)}) collective-permute-start(bf16[2,96,640]{2,1,0:T(8,128)(2,1)S(1)} %get-tuple-element.175), channel_id=1, source_target_pairs={{0,24},{1,25},{2,26},{3,27},{4,28},{5,29},{6,30},{7,31},{8,16},{9,... | collective-permute-start | bytes 737288 | tf_op jit(solution)/shard_map/ppermute | solution.py:722
  314.3 14.5 %copy-start.17 = (bf16[2,96,640]{2,1,0:T(8,128)(2,1)}, bf16[2,96,640]{2,1,0:T(8,128)(2,1)S(1)}, u32[]{:S(2)}) copy-start(bf16[2,96,640]{2,1,0:T(8,128)(2,1)S(1)} %add_convert_fusion.8) | copy-start | bytes 737284
  314.3 42.1 %collective-permute-start.31 = (bf16[2,96,640]{2,1,0:T(8,128)(2,1)S(1)}, bf16[2,96,640]{2,1,0:T(8,128)(2,1)}, u32[]{:S(2)}, u32[]{:S(2)}) collective-permute-start(bf16[2,96,640]{2,1,0:T(8,128)(2,1)S(1)} %add_convert_fusion.8), channel_id=1, source_target_pairs={{0,2},{1,3},{2,0},{3,1},{4,6},{5,7},{6,4},{7,5},{8,10},{9,11},{10,... | collective-permute-start | bytes 737288 | tf_op jit(solution)/shard_map/ppermute | solution.py:722
  326.3 31.4 %copy-start.8 = (f32[768,768]{1,0:T(8,128)S(1)}, f32[768,768]{1,0:T(8,128)}, u32[]{:S(2)}) copy-start(f32[768,768]{1,0:T(8,128)} %get-tuple-element.147) | copy-start | bytes 7077892
  357.6 3.7 collective-permute-start.33
  361.4 8.0 %collective-permute-start.34 = (bf16[2,96,640]{2,1,0:T(8,128)(2,1)S(1)}, bf16[2,96,640]{2,1,0:T(8,128)(2,1)S(1)}, u32[]{:S(2)}, u32[]{:S(2)}) collective-permute-start(bf16[2,96,640]{2,1,0:T(8,128)(2,1)S(1)} %maximum_select_fusion.4), channel_id=1, source_target_pairs={{0,1},{1,0},{2,3},{3,2},{4,5},{5,4},{6,7},{7,6},{8,9},{9,8},{10,11... | collective-permute-start | bytes 737288 | tf_op jit(solution)/shard_map/ppermute | solution.py:722
  (18 other events, 36.6 us)
Sparse Core Ops, SparseCore 0:
  10.5 75.1 all-gather.5
  159.6 74.1 reduce-scatter.2
  236.2 31.8 reduce-scatter.4
  288.5 51.2 all-gather.3
where the time goes:
time: 385 us; the launch traced here: 379 us
  Pallas kernels  172 us (45%)
  waiting for transfers between devices  96.2 us (25%)
  starting transfers between devices  55.3 us (14%)
  other arithmetic  25.4 us (7%)
  local copies, waits for them, and re-layouts  14.9 us (4%)
  between operations  14.8 us (4%)
    ppermute x35, waiting for transfers between devices, send(): return lax.ppermute(value, axes, pairs)  91 us
    pallas_call x2, Pallas kernels, attend_backward(): pl.pallas_call(functools.partial(backward_body, heads, top), grid_spec=pl...  66.1 us
    ppermute x35, starting transfers between devices, send(): return lax.ppermute(value, axes, pairs)  55.1 us
    pallas_call x1, Pallas kernels, hidden_layer(): pl.pallas_call(functools.partial(hidden_body, groups, rows), grid_spec=pl...  39 us
    pallas_call x1, Pallas kernels, attend_forward(): pl.pallas_call(functools.partial(forward_body, heads), grid_spec=pltpu.Pr...  28.5 us
    pallas_call x2, Pallas kernels, project(): pl.pallas_call(functools.partial(project_body, count), grid_spec=pltpu.Pr...  16.5 us
    pallas_call x2, Pallas kernels, final_norm(): pl.pallas_call(functools.partial(final_body, owner), grid_spec=pltpu.Pref...  12 us
    pallas_call x2, Pallas kernels, project_grad(): pl.pallas_call(project_grad_body, grid=(2,), in_specs=[pl.BlockSpec((cols...  10 us
  transfers between devices with their start and end apart: 39, of which 15 were waited for; matrix products, arithmetic and copies ran while one was open for 8% of the time, Pallas kernels for 35%

commit v1 on v0

--- a/solution.py
+++ b/solution.py
@@ -40,8 +40,12 @@
     )
 
 
-def params(*semantics):
-    return pltpu.CompilerParams(dimension_semantics=semantics, vmem_limit_bytes=VMEM_LIMIT)
+def in_hbm(*values):
+    return [pltpu.with_memory_space_constraint(v, pltpu.HBM) for v in values]
+
+
+def params(*semantics, limit=VMEM_LIMIT):
+    return pltpu.CompilerParams(dimension_semantics=semantics, vmem_limit_bytes=limit)
 
 
 def whole(shape):
@@ -87,7 +91,7 @@
 
     in_specs = [src(w, f) for w in range(count) for f in (1, 0)] + [whole(wt.shape)]
     aliases = {}
-    args = [info, *sources, wt]
+    args = [info, *in_hbm(*sources), wt]
     if carried is not None:
         in_specs += [pl.BlockSpec(memory_space=pl.ANY)] * 2
         aliases = {2 * count + 2: 0, 2 * count + 3: 1}
@@ -372,7 +376,7 @@
             bytes_accessed=20 * width * length,
         ),
         name="attention_backward",
-    )(info, packed, *outs, *grads, logsum, wt, *more)
+    )(info, packed, *in_hbm(*outs, *grads), logsum, wt, *more)
 
 
 def project_grad_body(*refs):
@@ -413,7 +417,7 @@
         out_specs=pl.BlockSpec(out.shape, lambda s: (0, 0)),
         out_shape=out,
         scratch_shapes=[pltpu.VMEM((cols, model), F32)],
-        compiler_params=params("arbitrary"),
+        compiler_params=params("arbitrary", limit=24 << 20),
         cost_estimate=pl.CostEstimate(
             flops=2 * cols * span * model, transcendentals=0, bytes_accessed=2 * span * (cols + model)
         ),
@@ -622,7 +626,7 @@
             bytes_accessed=4 * weights.size + 12 * size * model,
         ),
         name="hidden_layer",
-    )(info, tok, cot, *merged, wt, weights, weights, weights)
+    )(info, *in_hbm(tok, cot, *merged), wt, weights, weights, weights)
 
 
 def final_body(owner, info, tok, p0, p1, p2, resid_grad, vec_ref, before, *rest):
@@ -679,7 +683,7 @@
             flops=size * model, transcendentals=size, bytes_accessed=size * model
         ),
         name="final_norm",
-    )(info, tokens, *parts, resid_grad, wt, before, *more)
+    )(info, *in_hbm(tokens, *parts, resid_grad), wt, before, *more)
 
 
 def together(*values):

time: 385 us -> 388 us (level)
  Pallas kernels: 172 us -> 167 us
  local copies, waits for them, and re-layouts: 14.9 us -> 19.3 us
    pallas_call x2, Pallas kernels: 10 us -> 4.44 us  [project_grad(): pl.pallas_call(project_grad_body, grid=(2,), in_specs=[pl.BlockSpec((cols...]
    unnamed x60 -> x62, local copies, waits for them, and re-layouts: 5.83 us -> 10.3 us
  transfers between devices with their start and end apart: 39 -> 39, of which waited for: 15 -> 15; matrix products, arithmetic and copies ran while one was open for 8% -> 9% of each run, Pallas kernels for 35% -> 33%
where the time goes in v1:
time: 388 us; the launch traced here: 382 us
  Pallas kernels  167 us (43%)
  waiting for transfers between devices  99.2 us (26%)
  starting transfers between devices  53.3 us (14%)
  other arithmetic  28.4 us (7%)
  local copies, waits for them, and re-layouts  19.3 us (5%)
  between operations  14.8 us (4%)
    ppermute x35, waiting for transfers between devices, send(): return lax.ppermute(value, axes, pairs)  93.5 us
    pallas_call x2, Pallas kernels, attend_backward(): pl.pallas_call(functools.partial(backward_body, heads, top), grid_spec=pl...  65.9 us
    ppermute x35, starting transfers between devices, send(): return lax.ppermute(value, axes, pairs)  53.1 us
    pallas_call x1, Pallas kernels, hidden_layer(): pl.pallas_call(functools.partial(hidden_body, groups, rows), grid_spec=pl...  39 us
    pallas_call x1, Pallas kernels, attend_forward(): pl.pallas_call(functools.partial(forward_body, heads), grid_spec=pltpu.Pr...  28.5 us
    pallas_call x2, Pallas kernels, project(): pl.pallas_call(functools.partial(project_body, count), grid_spec=pltpu.Pr...  16.6 us
    pallas_call x2, Pallas kernels, final_norm(): pl.pallas_call(functools.partial(final_body, owner), grid_spec=pltpu.Pref...  12.2 us
    unnamed x62, local copies, waits for them, and re-layouts  10.3 us
  transfers between devices with their start and end apart: 39, of which 15 were waited for; matrix products, arithmetic and copies ran while one was open for 9% of the time, Pallas kernels for 33%

profile of v1, /device:TPU:0, one launch (start us, length us, event | category | flops | bytes accessed | tf_op | source)
XLA Modules:
  0.0 381.7 jit_solution(11018024926594116652)
XLA Ops:
  10.2 3.0 collective-permute-start
  13.2 1.6 reshape.60
  19.2 1.6 collective-permute-start.4
  20.8 1.5 collective-permute-start.2
  22.8 9.5 %collective-permute-done.4 = bf16[2,96,640]{2,1,0:T(8,128)(2,1)S(1)} collective-permute-done((bf16[2,96,640]{2,1,0:T(8,128)(2,1)S(1)}, bf16[2,96,640]{2,1,0:T(8,128)(2,1)S(1)}, u32[]{:S(2)}, u32[]{:S(2)}) %collective-permute-start.4) | collective-permute-done | bytes 245792 | tf_op jit(solution)/shard_map/ppermute | solution.py:726
  32.4 10.6 %collective-permute-done.2 = bf16[2,96,640]{2,1,0:T(8,128)(2,1)S(1)} collective-permute-done((bf16[2,96,640]{2,1,0:T(8,128)(2,1)S(1)}, bf16[2,96,640]{2,1,0:T(8,128)(2,1)S(1)}, u32[]{:S(2)}, u32[]{:S(2)}) %collective-permute-start.2) | collective-permute-done | bytes 245792 | tf_op jit(solution)/shard_map/ppermute | solution.py:726
  44.3 1.7 collective-permute-start.5
  46.6 2.3 copy.44
  49.9 11.3 %norm_project.2 = (bf16[576,3072]{1,0:T(8,128)(2,1)}, bf16[3072,768]{1,0:T(8,128)(2,1)}) custom-call(s32[4]{0:T(128)} %pad_add_fusion.2.info, bf16[768,768]{1,0:T(8,128)(2,1)} %bitcast.61, bf16[768,768]{1,0:T(8,128)(2,1)} %collective-permute-done.6.refs_1_, bf16[768,768]{1,0:T(8,128)(2,1)} %copy-done.4, bf16[768,768]{1,0:T(8,128)(2,1)} %copy-done.9, ...), custom_call_target="tpu_custom_call" | custom-call | flops 2038431744 | bytes 10616832 | tf_op jit(solution)/shard_map/norm_project/pallas_call | solution.py:99
  61.2 3.7 collective-permute-start.8
  68.6 5.3 %norm_project.3 = (bf16[576,3072]{1,0:T(8,128)(2,1)}, bf16[3072,768]{1,0:T(8,128)(2,1)}) custom-call(s32[2]{0:T(128)} %pad_add_fusion.1.info, bf16[768,768]{1,0:T(8,128)(2,1)} %copy-done.14, bf16[768,768]{1,0:T(8,128)(2,1)} %collective-permute-done.5.refs_1_, bf16[640,768]{1,0:T(8,128)(2,1)} %bitcast.55, ...), custom_call_target="tpu_custom_call", output_to_operand_aliasing={{0}: (4, {}), {1}: (5, {})} | custom-call | flops 679477248 | bytes 3538944 | tf_op jit(solution)/shard_map/norm_project/pallas_call | solution.py:99
  74.0 28.5 %attention_forward.1 = (bf16[192,768]{1,0:T(8,128)(2,1)}, bf16[192,768]{1,0:T(8,128)(2,1)}, bf16[192,768]{1,0:T(8,128)(2,1)}, bf16[192,768]{1,0:T(8,128)(2,1)}, f32[8,3072]{1,0:T(8,128)}) custom-call(s32[3]{0:T(128)} %pad_add_fusion.info, bf16[576,3072]{1,0:T(8,128)(2,1)} %get-tuple-element.92.packed), custom_call_target="tpu_custom_call" | custom-call | flops 589824 | bytes 589824 | tf_op jit(solution)/shard_map/attention_forward/pallas_call | solution.py:207
  106.9 5.6 %collective-permute-done.10.m1 = bf16[192,768]{1,0:T(8,128)(2,1)S(1)} collective-permute-done((bf16[192,768]{1,0:T(8,128)(2,1)}, bf16[192,768]{1,0:T(8,128)(2,1)S(1)}, u32[]{:S(2)}, u32[]{:S(2)}) %collective-permute-start.10) | collective-permute-done | bytes 294944 | tf_op jit(solution)/shard_map/ppermute | solution.py:726
  112.6 5.8 %collective-permute-done.12.m3 = bf16[192,768]{1,0:T(8,128)(2,1)} collective-permute-done((bf16[192,768]{1,0:T(8,128)(2,1)}, bf16[192,768]{1,0:T(8,128)(2,1)}, u32[]{:S(2)}, u32[]{:S(2)}) %collective-permute-start.12) | collective-permute-done | bytes 294944 | tf_op jit(solution)/shard_map/ppermute | solution.py:726
  118.4 39.0 %hidden_layer.1 = (bf16[768,768]{1,0:T(8,128)(2,1)}, f32[768,768]{1,0:T(8,128)}, bf16[192,768]{1,0:T(8,128)(2,1)}, bf16[192,768]{1,0:T(8,128)(2,1)}, bf16[192,76...) custom-call(s32[3]{0:T(128)} %pad_add_fusion.info, ...), custom_call_target="tpu_custom_call" | custom-call | flops 24461180928 | bytes 28311552 | tf_op jit(solution)/shard_map/hidden_layer/pallas_call | solution.py:585
  159.6 7.0 %collective-permute-done.13.g3 = bf16[192,768]{1,0:T(8,128)(2,1)S(1)} collective-permute-done((bf16[192,768]{1,0:T(8,128)(2,1)}, bf16[192,768]{1,0:T(8,128)(2,1)S(1)}, u32[]{:S(2)}, u32[]{:S(2)}) %collective-permute-start.13) | collective-permute-done | bytes 294944 | tf_op jit(solution)/shard_map/ppermute | solution.py:726
  166.6 1.7 collective-permute-start.16
  168.3 3.8 fusion.5
  172.1 1.8 collective-permute-start.18
  176.7 43.1 %attention_backward.2 = (bf16[768,768]{1,0:T(8,128)(2,1)}, bf16[768,768]{1,0:T(8,128)(2,1)}, bf16[576,1536]{1,0:T(8,128)(2,1)}, f32[3,1536,64]{2,1,0:T(8,128)}, f32[3,1536,64]{2,1,0:T(8,128)}) custom-call(s32[3]{0:T(128)} %pad_add_fusion.info, bf16[576,3072]{1,0:T(8,128)(2,1)} %get-tuple-element.92.packed, bf16[192,768]{1,0:T(8,128)(2,1)} %get-tuple-element.97.m0.o0, ...), custom_call_target="tpu_custom_call" | custom-call | flops 158544691200 | bytes 11796480 | tf_op jit(solution)/shard_map/attention_backward/pallas_call | solution.py:355
  219.9 2.1 collective-permute-start.21
  222.0 2.2 add_convert_fusion.2
  224.4 2.9 add_convert_fusion.1
  227.3 1.7 collective-permute-start.22
  228.9 2.1 project_grad.2.refs_2_
  231.0 3.0 reduce-scatter.3.cloned.1.call-done
  234.0 2.4 pad_maximum_fusion
  236.4 22.8 %attention_backward.3 = (bf16[768,768]{1,0:T(8,128)(2,1)}, bf16[768,768]{1,0:T(8,128)(2,1)}, bf16[576,1536]{1,0:T(8,128)(2,1)}) custom-call(s32[3]{0:T(128)} %pad_add_fusion.info, bf16[576,3072]{1,0:T(8,128)(2,1)} %get-tuple-element.92.packed, bf16[192,768]{1,0:T(8,128)(2,1)} %get-tuple-element.97.m0.o0, bf16[192,768]{1,0:T(8,128)(2,1)} %get-tuple-element.98.o1, ...), custom_call_target="tpu_custom_call" | custom-call | flops 67947724800 | bytes 11796480 | tf_op jit(solution)/shard_map/attention_backward/pallas_call | solution.py:355
  260.5 5.1 %collective-permute-start.26 = (bf16[768,768]{1,0:T(8,128)(2,1)}, bf16[768,768]{1,0:T(8,128)(2,1)}, u32[]{:S(2)}, u32[]{:S(2)}) collective-permute-start(bf16[768,768]{1,0:T(8,128)(2,1)} %get-tuple-element.137.p0), channel_id=1, source_target_pairs={{0,4},{1,5},{2,6},{3,7},{8,12},{9,13},{10,14},{11,15},{16,20},{17,... | collective-permute-start | bytes 3538952 | tf_op jit(solution)/shard_map/ppermute | solution.py:726
  265.6 2.7 reduce-scatter.5.cloned.1.call-done
  268.3 3.0 add_convert_fusion
  271.4 1.9 collective-permute-start.25
  273.3 1.5 collective-permute-start.23
  274.8 5.4 %final_norm.2 = (f32[768,768]{1,0:T(8,128)}, bf16[768,768]{1,0:T(8,128)(2,1)}, f32[8,768]{1,0:T(8,128)}) custom-call(s32[3]{0:T(128)} %pad_add_fusion.info, bf16[768,768]{1,0:T(8,128)(2,1)} %broadcast_select_fusion.1.tok, bf16[768,768]{1,0:T(8,128)(2,1)} %get-tuple-element.137.p0, bf16[768,768]{1,0:T(8,128)(2,1)} %collective-permute-done.26.p1, ...), custom_call_target="tpu_custom_call" | custom-call | flops 589824 | bytes 589824 | tf_op jit(solution)/shard_map/final_norm/pallas_call | solution.py:666
  280.2 2.3 copy-done.1
  282.5 1.5 copy-done.2
  284.0 2.4 project_grad.3
  286.4 3.4 collective-permute-done.25.p2
  290.6 6.8 %final_norm.3 = (f32[768,768]{1,0:T(8,128)}, bf16[768,768]{1,0:T(8,128)(2,1)}, f32[8,768]{1,0:T(8,128)}) custom-call(s32[3]{0:T(128)} %pad_add_fusion.info, bf16[768,768]{1,0:T(8,128)(2,1)} %broadcast_select_fusion.1.tok, bf16[768,768]{1,0:T(8,128)(2,1)} %get-tuple-element.125.p0, bf16[768,768]{1,0:T(8,128)(2,1)} %collective-permute-done.23.p1, ...), custom_call_target="tpu_custom_call" | custom-call | flops 589824 | bytes 589824 | tf_op jit(solution)/shard_map/final_norm/pallas_call | solution.py:666
  297.4 1.7 collective-permute-start.32
  300.3 1.9 collective-permute-start.28
  303.8 4.6 %collective-permute-done.28 = bf16[2,96,640]{2,1,0:T(8,128)(2,1)S(1)} collective-permute-done((bf16[2,96,640]{2,1,0:T(8,128)(2,1)S(1)}, bf16[2,96,640]{2,1,0:T(8,128)(2,1)S(1)}, u32[]{:S(2)}, u32[]{:S(2)}) %collective-permute-start.28) | collective-permute-done | bytes 245792 | tf_op jit(solution)/shard_map/ppermute | solution.py:726
  308.5 7.5 %collective-permute-done.29 = bf16[2,96,640]{2,1,0:T(8,128)(2,1)S(1)} collective-permute-done((bf16[2,96,640]{2,1,0:T(8,128)(2,1)S(1)}, bf16[2,96,640]{2,1,0:T(8,128)(2,1)S(1)}, u32[]{:S(2)}, u32[]{:S(2)}) %collective-permute-start.29) | collective-permute-done | bytes 245792 | tf_op jit(solution)/shard_map/ppermute | solution.py:726
  316.8 9.2 %collective-permute-start.31 = (bf16[2,96,640]{2,1,0:T(8,128)(2,1)S(1)}, bf16[2,96,640]{2,1,0:T(8,128)(2,1)}, u32[]{:S(2)}, u32[]{:S(2)}) collective-permute-start(bf16[2,96,640]{2,1,0:T(8,128)(2,1)S(1)} %add_convert_fusion.8), channel_id=1, source_target_pairs={{0,2},{1,3},{2,0},{3,1},{4,6},{5,7},{6,4},{7,5},{8,10},{9,11},{10,... | collective-permute-start | bytes 737288 | tf_op jit(solution)/shard_map/ppermute | solution.py:726
  326.1 2.6 select_bitcast_fusion.1
  328.6 30.8 %collective-permute-done.31 = bf16[2,96,640]{2,1,0:T(8,128)(2,1)} collective-permute-done((bf16[2,96,640]{2,1,0:T(8,128)(2,1)S(1)}, bf16[2,96,640]{2,1,0:T(8,128)(2,1)}, u32[]{:S(2)}, u32[]{:S(2)}) %collective-permute-start.31) | collective-permute-done | bytes 245792 | tf_op jit(solution)/shard_map/ppermute | solution.py:726
  360.7 1.7 select_bitcast_fusion
  365.5 6.8 %collective-permute-done.34 = bf16[2,96,640]{2,1,0:T(8,128)(2,1)S(1)} collective-permute-done((bf16[2,96,640]{2,1,0:T(8,128)(2,1)S(1)}, bf16[2,96,640]{2,1,0:T(8,128)(2,1)S(1)}, u32[]{:S(2)}, u32[]{:S(2)}) %collective-permute-start.34) | collective-permute-done | bytes 245792 | tf_op jit(solution)/shard_map/ppermute | solution.py:726
  (149 shorter events, 36.6 us)
Async XLA Ops:
  7.2 111.1 %all-gather.6.cloned.1.call-start = ((), (), s32[]{:S(2)}) async-start(), calls=%async_computation.5 | async-start | bytes 11943936 | tf_op jit(solution)/shard_map/all_gather | solution.py:792
  9.6 224.4 %reduce-scatter.3.cloned.1.call-start = ((), (), s32[]{:S(2)}) async-start(), calls=%async_computation.2 | async-start | bytes 6635520 | tf_op jit(solution)/shard_map/reduce_scatter | solution.py:848
  10.2 34.1 %collective-permute-start = (bf16[768,768]{1,0:T(8,128)(2,1)S(1)}, bf16[768,768]{1,0:T(8,128)(2,1)S(1)}, u32[]{:S(2)}, u32[]{:S(2)}) collective-permute-start(bf16[768,768]{1,0:T(8,128)(2,1)S(1)} %bitcast.62), channel_id=1, source_target_pairs={{0,1},{1,0},{2,4},{3,5},{4,2},{5,3},{6,7},{7,6},{8,9},{9,8},{10,12... | collective-permute-start | bytes 3538952 | tf_op jit(solution)/shard_map/ppermute | solution.py:726
  17.0 2.2 collective-permute-start.1
  19.2 13.1 %collective-permute-start.4 = (bf16[2,96,640]{2,1,0:T(8,128)(2,1)S(1)}, bf16[2,96,640]{2,1,0:T(8,128)(2,1)S(1)}, u32[]{:S(2)}, u32[]{:S(2)}) collective-permute-start(bf16[2,96,640]{2,1,0:T(8,128)(2,1)S(1)} %maximum_select_fusion.3), channel_id=1, source_target_pairs={{0,8},{1,9},{2,10},{3,11},{4,12},{5,13},{6,14},{7,15},{8,0},{9,1},... | collective-permute-start | bytes 737288 | tf_op jit(solution)/shard_map/ppermute | solution.py:726
  20.8 22.3 %collective-permute-start.2 = (bf16[2,96,640]{2,1,0:T(8,128)(2,1)S(1)}, bf16[2,96,640]{2,1,0:T(8,128)(2,1)S(1)}, u32[]{:S(2)}, u32[]{:S(2)}) collective-permute-start(bf16[2,96,640]{2,1,0:T(8,128)(2,1)S(1)} %maximum_select_fusion.3), channel_id=1, source_target_pairs={{0,24},{1,25},{2,26},{3,27},{4,28},{5,29},{6,30},{7,31},{8,16},{9,... | collective-permute-start | bytes 737288 | tf_op jit(solution)/shard_map/ppermute | solution.py:726
  22.3 20.8 %collective-permute-start.3 = (bf16[2,96,640]{2,1,0:T(8,128)(2,1)S(1)}, bf16[2,96,640]{2,1,0:T(8,128)(2,1)S(1)}, u32[]{:S(2)}, u32[]{:S(2)}) collective-permute-start(bf16[2,96,640]{2,1,0:T(8,128)(2,1)S(1)} %maximum_select_fusion.3), channel_id=1, source_target_pairs={{0,16},{1,17},{2,18},{3,19},{4,20},{5,21},{6,22},{7,23},{8,24},{9,... | collective-permute-start | bytes 737288 | tf_op jit(solution)/shard_map/ppermute | solution.py:726
  22.8 26.1 %collective-permute-start.6 = (bf16[768,768]{1,0:T(8,128)(2,1)S(1)}, bf16[768,768]{1,0:T(8,128)(2,1)}, u32[]{:S(2)}, u32[]{:S(2)}) collective-permute-start(bf16[768,768]{1,0:T(8,128)(2,1)S(1)} %bitcast.63), channel_id=1, source_target_pairs={{0,4},{1,5},{2,6},{3,7},{4,0},{5,1},{6,2},{7,3},{8,12},{9,13},{10,... | collective-permute-start | bytes 3538952 | tf_op jit(solution)/shard_map/ppermute | solution.py:726
  44.3 4.6 %collective-permute-start.7 = (bf16[768,768]{1,0:T(8,128)(2,1)S(1)}, bf16[768,768]{1,0:T(8,128)(2,1)S(1)}, u32[]{:S(2)}, u32[]{:S(2)}) collective-permute-start(bf16[768,768]{1,0:T(8,128)(2,1)S(1)} %collective-permute-done.refs_2_.refs_5_), channel_id=1, source_target_pairs={{0,4},{1,5},{2,6},{3,7},{4,0},{5,1},{6,2},{7,3},{8,12},{9,13},{10,... | collective-permute-start | bytes 3538952 | tf_op jit(solution)/shard_map/ppermute | solution.py:726
  44.3 16.9 %collective-permute-start.5 = (bf16[768,768]{1,0:T(8,128)(2,1)S(1)}, bf16[768,768]{1,0:T(8,128)(2,1)}, u32[]{:S(2)}, u32[]{:S(2)}) collective-permute-start(bf16[768,768]{1,0:T(8,128)(2,1)S(1)} %collective-permute-done.refs_2_.refs_5_), channel_id=1, source_target_pairs={{2,3},{3,2},{4,5},{5,4},{10,11},{11,10},{12,13},{13,12},{18,19},{1... | collective-permute-start | bytes 3538952 | tf_op jit(solution)/shard_map/ppermute | solution.py:726
  61.2 6.4 %collective-permute-start.8 = (bf16[768,768]{1,0:T(8,128)(2,1)}, bf16[768,768]{1,0:T(8,128)(2,1)S(1)}, u32[]{:S(2)}, u32[]{:S(2)}) collective-permute-start(bf16[768,768]{1,0:T(8,128)(2,1)} %collective-permute-done.5.refs_1_), channel_id=1, source_target_pairs={{0,4},{1,5},{2,6},{3,7},{4,0},{5,1},{6,2},{7,3},{8,12},{9,13},{10,... | collective-permute-start | bytes 3538952 | tf_op jit(solution)/shard_map/ppermute | solution.py:726
  64.9 40.9 %collective-permute-start.9 = (bf16[768,768]{1,0:T(8,128)(2,1)}, bf16[768,768]{1,0:T(8,128)(2,1)S(1)}, u32[]{:S(2)}, u32[]{:S(2)}) collective-permute-start(bf16[768,768]{1,0:T(8,128)(2,1)} %bitcast.68), channel_id=1, source_target_pairs={{2,4},{3,5},{4,2},{5,3},{10,12},{11,13},{12,10},{13,11},{18,20},{1... | collective-permute-start | bytes 3538952 | tf_op jit(solution)/shard_map/ppermute | solution.py:726
  74.0 30.7 %copy-start.5 = (bf16[768,768]{1,0:T(8,128)(2,1)S(1)}, bf16[768,768]{1,0:T(8,128)(2,1)}, u32[]{:S(2)}) copy-start(bf16[768,768]{1,0:T(8,128)(2,1)} %copy-done.4) | copy-start | bytes 3538948
  74.0 30.7 %copy-start.8 = (bf16[1,768,768]{2,1,0:T(8,128)(2,1)S(1)}, bf16[1,768,768]{2,1,0:T(8,128)(2,1)}, u32[]{:S(2)}) copy-start(bf16[1,768,768]{2,1,0:T(8,128)(2,1)} %param.11) | copy-start | bytes 3538948
  102.5 10.1 %collective-permute-start.10 = (bf16[192,768]{1,0:T(8,128)(2,1)}, bf16[192,768]{1,0:T(8,128)(2,1)S(1)}, u32[]{:S(2)}, u32[]{:S(2)}) collective-permute-start(bf16[192,768]{1,0:T(8,128)(2,1)} %get-tuple-element.98.o1), channel_id=1, source_target_pairs={{0,1},{1,0},{2,3},{3,2},{4,5},{5,4},{6,7},{7,6},{8,9},{9,8},{10,11... | collective-permute-start | bytes 884744 | tf_op jit(solution)/shard_map/ppermute | solution.py:726
  102.5 10.1 %collective-permute-start.11 = (bf16[192,768]{1,0:T(8,128)(2,1)}, bf16[192,768]{1,0:T(8,128)(2,1)S(1)}, u32[]{:S(2)}, u32[]{:S(2)}) collective-permute-start(bf16[192,768]{1,0:T(8,128)(2,1)} %get-tuple-element.99.o2), channel_id=1, source_target_pairs={{0,4},{1,5},{2,6},{3,7},{4,0},{5,1},{6,2},{7,3},{8,12},{9,13},{10,... | collective-permute-start | bytes 884744 | tf_op jit(solution)/shard_map/ppermute | solution.py:726
  103.2 15.2 %collective-permute-start.12 = (bf16[192,768]{1,0:T(8,128)(2,1)}, bf16[192,768]{1,0:T(8,128)(2,1)}, u32[]{:S(2)}, u32[]{:S(2)}) collective-permute-start(bf16[192,768]{1,0:T(8,128)(2,1)} %get-tuple-element.100.o3), channel_id=1, source_target_pairs={{0,5},{1,4},{2,7},{3,6},{4,1},{5,0},{6,3},{7,2},{8,13},{9,12},{10,... | collective-permute-start | bytes 884744 | tf_op jit(solution)/shard_map/ppermute | solution.py:726
  112.6 5.8 %copy-start.26 = (bf16[192,768]{1,0:T(8,128)(2,1)}, bf16[192,768]{1,0:T(8,128)(2,1)S(1)}, u32[]{:S(2)}) copy-start(bf16[192,768]{1,0:T(8,128)(2,1)S(1)} %collective-permute-done.10.m1) | copy-start | bytes 884740
  112.6 5.8 %copy-start.27 = (bf16[192,768]{1,0:T(8,128)(2,1)}, bf16[192,768]{1,0:T(8,128)(2,1)S(1)}, u32[]{:S(2)}) copy-start(bf16[192,768]{1,0:T(8,128)(2,1)S(1)} %collective-permute-done.11.m2) | copy-start | bytes 884740
  157.4 11.0 %collective-permute-start.17 = (bf16[4,384,768]{2,1,0:T(8,128)(2,1)}, bf16[4,384,768]{2,1,0:T(8,128)(2,1)}, u32[]{:S(2)}, u32[]{:S(2)}) collective-permute-start(bf16[4,384,768]{2,1,0:T(8,128)(2,1)} %get-tuple-element.112), channel_id=1, source_target_pairs={{0,4},{1,5},{2,6},{3,7},{4,0},{5,1},{6,2},{7,3},{8,12},{9,13},{10,... | collective-permute-start | bytes 7077896 | tf_op jit(solution)/shard_map/ppermute | solution.py:726
  157.6 9.0 %collective-permute-start.13 = (bf16[192,768]{1,0:T(8,128)(2,1)}, bf16[192,768]{1,0:T(8,128)(2,1)S(1)}, u32[]{:S(2)}, u32[]{:S(2)}) collective-permute-start(bf16[192,768]{1,0:T(8,128)(2,1)} %get-tuple-element.102), channel_id=1, source_target_pairs={{0,5},{1,4},{2,7},{3,6},{4,1},{5,0},{6,3},{7,2},{8,13},{9,12},{10,... | collective-permute-start | bytes 884744 | tf_op jit(solution)/shard_map/ppermute | solution.py:726
  158.1 17.0 %collective-permute-start.14 = (bf16[192,768]{1,0:T(8,128)(2,1)}, bf16[192,768]{1,0:T(8,128)(2,1)S(1)}, u32[]{:S(2)}, u32[]{:S(2)}) collective-permute-start(bf16[192,768]{1,0:T(8,128)(2,1)} %get-tuple-element.105), channel_id=1, source_target_pairs={{0,1},{1,0},{2,3},{3,2},{4,5},{5,4},{6,7},{7,6},{8,9},{9,8},{10,11... | collective-permute-start | bytes 884744 | tf_op jit(solution)/shard_map/ppermute | solution.py:726
  159.6 16.5 %collective-permute-start.15 = (bf16[192,768]{1,0:T(8,128)(2,1)}, bf16[192,768]{1,0:T(8,128)(2,1)S(1)}, u32[]{:S(2)}, u32[]{:S(2)}) collective-permute-start(bf16[192,768]{1,0:T(8,128)(2,1)} %get-tuple-element.106), channel_id=1, source_target_pairs={{0,4},{1,5},{2,6},{3,7},{4,0},{5,1},{6,2},{7,3},{8,12},{9,13},{10,... | collective-permute-start | bytes 884744 | tf_op jit(solution)/shard_map/ppermute | solution.py:726
  159.6 8.8 %copy-start.12 = (bf16[4,384,768]{2,1,0:T(8,128)(2,1)S(1)}, bf16[4,384,768]{2,1,0:T(8,128)(2,1)}, u32[]{:S(2)}) copy-start(bf16[4,384,768]{2,1,0:T(8,128)(2,1)} %get-tuple-element.111) | copy-start | bytes 7077892
  159.6 108.7 %reduce-scatter.5.cloned.1.call-start = ((), (), s32[]{:S(2)}) async-start(), calls=%async_computation.3 | async-start | bytes 1658880 | tf_op jit(solution)/shard_map/reduce_scatter | solution.py:873
  166.6 5.5 %copy-start.23 = (bf16[192,768]{1,0:T(8,128)(2,1)}, bf16[192,768]{1,0:T(8,128)(2,1)S(1)}, u32[]{:S(2)}) copy-start(bf16[192,768]{1,0:T(8,128)(2,1)S(1)} %collective-permute-done.13.g3) | copy-start | bytes 884740
  166.6 53.2 %collective-permute-start.16 = (bf16[768,768]{1,0:T(8,128)(2,1)}, bf16[768,768]{1,0:T(8,128)(2,1)}, u32[]{:S(2)}, u32[]{:S(2)}) collective-permute-start(bf16[768,768]{1,0:T(8,128)(2,1)} %get-tuple-element.103), channel_id=1, source_target_pairs={{2,4},{3,5},{4,2},{5,3},{10,12},{11,13},{12,10},{13,11},{18,20},{1... | collective-permute-start | bytes 3538952 | tf_op jit(solution)/shard_map/ppermute | solution.py:726
  172.1 47.8 %collective-permute-start.18 = (bf16[384,768]{1,0:T(8,128)(2,1)}, bf16[384,768]{1,0:T(8,128)(2,1)}, u32[]{:S(2)}, u32[]{:S(2)}) collective-permute-start(bf16[384,768]{1,0:T(8,128)(2,1)} %get-tuple-element.168), channel_id=1, source_target_pairs={{0,8},{1,9},{2,10},{3,11},{4,12},{5,13},{6,14},{7,15},{8,0},{9,1},... | collective-permute-start | bytes 1769480 | tf_op jit(solution)/shard_map/ppermute | solution.py:726
  173.9 46.0 %collective-permute-start.19 = (bf16[384,768]{1,0:T(8,128)(2,1)}, bf16[384,768]{1,0:T(8,128)(2,1)}, u32[]{:S(2)}, u32[]{:S(2)}) collective-permute-start(bf16[384,768]{1,0:T(8,128)(2,1)} %get-tuple-element.167), channel_id=1, source_target_pairs={{0,16},{1,17},{2,18},{3,19},{4,20},{5,21},{6,22},{7,23},{8,24},{9,... | collective-permute-start | bytes 1769480 | tf_op jit(solution)/shard_map/ppermute | solution.py:726
  175.1 44.8 %collective-permute-start.20 = (bf16[384,768]{1,0:T(8,128)(2,1)}, bf16[384,768]{1,0:T(8,128)(2,1)}, u32[]{:S(2)}, u32[]{:S(2)}) collective-permute-start(bf16[384,768]{1,0:T(8,128)(2,1)} %get-tuple-element.166), channel_id=1, source_target_pairs={{0,24},{1,25},{2,26},{3,27},{4,28},{5,29},{6,30},{7,31},{8,16},{9,... | collective-permute-start | bytes 1769480 | tf_op jit(solution)/shard_map/ppermute | solution.py:726
  176.7 45.3 %copy-start.13 = (bf16[384,768]{1,0:T(8,128)(2,1)S(1)}, bf16[384,768]{1,0:T(8,128)(2,1)}, u32[]{:S(2)}) copy-start(bf16[384,768]{1,0:T(8,128)(2,1)} %get-tuple-element.127) | copy-start | bytes 1769476
  219.9 4.5 %collective-permute-start.21 = (bf16[768,768]{1,0:T(8,128)(2,1)}, bf16[768,768]{1,0:T(8,128)(2,1)S(1)}, u32[]{:S(2)}, u32[]{:S(2)}) collective-permute-start(bf16[768,768]{1,0:T(8,128)(2,1)} %get-tuple-element.114), channel_id=1, source_target_pairs={{0,4},{1,5},{2,6},{3,7},{8,12},{9,13},{10,14},{11,15},{16,20},{17,... | collective-permute-start | bytes 3538952 | tf_op jit(solution)/shard_map/ppermute | solution.py:726
  222.0 6.9 %copy-start = (bf16[3072,768]{1,0:T(8,128)(2,1)S(1)}, bf16[3072,768]{1,0:T(8,128)(2,1)}, u32[]{:S(2)}) copy-start(bf16[3072,768]{1,0:T(8,128)(2,1)} %get-tuple-element.119.refs_1_) | copy-start | bytes 14155780
  227.3 32.0 %collective-permute-start.22 = (bf16[768,768]{1,0:T(8,128)(2,1)}, bf16[768,768]{1,0:T(8,128)(2,1)}, u32[]{:S(2)}, u32[]{:S(2)}) collective-permute-start(bf16[768,768]{1,0:T(8,128)(2,1)} %add_convert_fusion.1), channel_id=1, source_target_pairs={{4,5},{5,4},{6,7},{7,6},{12,13},{13,12},{14,15},{15,14},{20,21},{2... | collective-permute-start | bytes 3538952 | tf_op jit(solution)/shard_map/ppermute | solution.py:726
  236.4 123.0 %all-gather.4.cloned.1.call-start = ((), (), s32[]{:S(2)}) async-start(), calls=%async_computation.4 | async-start | bytes 1658880 | tf_op jit(solution)/shard_map/all_gather | solution.py:889
  259.2 6.4 %collective-permute-start.24 = (bf16[768,768]{1,0:T(8,128)(2,1)}, bf16[768,768]{1,0:T(8,128)(2,1)}, u32[]{:S(2)}, u32[]{:S(2)}) collective-permute-start(bf16[768,768]{1,0:T(8,128)(2,1)} %get-tuple-element.126), channel_id=1, source_target_pairs={{4,0},{5,1},{6,2},{7,3},{12,8},{13,9},{14,10},{15,11},{20,16},{21,... | collective-permute-start | bytes 3538952 | tf_op jit(solution)/shard_map/ppermute | solution.py:726
  260.5 14.3 %collective-permute-start.26 = (bf16[768,768]{1,0:T(8,128)(2,1)}, bf16[768,768]{1,0:T(8,128)(2,1)}, u32[]{:S(2)}, u32[]{:S(2)}) collective-permute-start(bf16[768,768]{1,0:T(8,128)(2,1)} %get-tuple-element.137.p0), channel_id=1, source_target_pairs={{0,4},{1,5},{2,6},{3,7},{8,12},{9,13},{10,14},{11,15},{16,20},{17,... | collective-permute-start | bytes 3538952 | tf_op jit(solution)/shard_map/ppermute | solution.py:726
  271.4 18.4 %collective-permute-start.25 = (bf16[768,768]{1,0:T(8,128)(2,1)}, bf16[768,768]{1,0:T(8,128)(2,1)}, u32[]{:S(2)}, u32[]{:S(2)}) collective-permute-start(bf16[768,768]{1,0:T(8,128)(2,1)} %add_convert_fusion), channel_id=1, source_target_pairs={{0,1},{1,0},{2,3},{3,2},{8,9},{9,8},{10,11},{11,10},{16,17},{17,16... | collective-permute-start | bytes 3538952 | tf_op jit(solution)/shard_map/ppermute | solution.py:726
  273.3 17.3 %collective-permute-start.23 = (bf16[768,768]{1,0:T(8,128)(2,1)}, bf16[768,768]{1,0:T(8,128)(2,1)}, u32[]{:S(2)}, u32[]{:S(2)}) collective-permute-start(bf16[768,768]{1,0:T(8,128)(2,1)} %get-tuple-element.125.p0), channel_id=1, source_target_pairs={{4,0},{5,1},{6,2},{7,3},{12,8},{13,9},{14,10},{15,11},{20,16},{21,... | collective-permute-start | bytes 3538952 | tf_op jit(solution)/shard_map/ppermute | solution.py:726
  289.8 26.2 %collective-permute-start.27 = (bf16[768,768]{1,0:T(8,128)(2,1)}, bf16[768,768]{1,0:T(8,128)(2,1)S(1)}, u32[]{:S(2)}, u32[]{:S(2)}) collective-permute-start(bf16[768,768]{1,0:T(8,128)(2,1)} %get-tuple-element.148), channel_id=1, source_target_pairs={{4,2},{5,3},{12,10},{13,11},{20,18},{21,19},{28,26},{29,27}} | collective-permute-start | bytes 3538952 | tf_op jit(solution)/shard_map/ppermute | solution.py:726
  297.4 31.2 %collective-permute-start.32 = (bf16[768,768]{1,0:T(8,128)(2,1)}, bf16[768,768]{1,0:T(8,128)(2,1)}, u32[]{:S(2)}, u32[]{:S(2)}) collective-permute-start(bf16[768,768]{1,0:T(8,128)(2,1)} %get-tuple-element.156), channel_id=1, source_target_pairs={{2,4},{3,5},{10,12},{11,13},{18,20},{19,21},{26,28},{27,29}} | collective-permute-start | bytes 3538952 | tf_op jit(solution)/shard_map/ppermute | solution.py:726
  300.3 8.2 %collective-permute-start.28 = (bf16[2,96,640]{2,1,0:T(8,128)(2,1)S(1)}, bf16[2,96,640]{2,1,0:T(8,128)(2,1)S(1)}, u32[]{:S(2)}, u32[]{:S(2)}) collective-permute-start(bf16[2,96,640]{2,1,0:T(8,128)(2,1)S(1)} %get-tuple-element.177), channel_id=1, source_target_pairs={{0,8},{1,9},{2,10},{3,11},{4,12},{5,13},{6,14},{7,15},{8,0},{9,1},... | collective-permute-start | bytes 737288 | tf_op jit(solution)/shard_map/ppermute | solution.py:726
  302.2 13.8 %collective-permute-start.29 = (bf16[2,96,640]{2,1,0:T(8,128)(2,1)S(1)}, bf16[2,96,640]{2,1,0:T(8,128)(2,1)S(1)}, u32[]{:S(2)}, u32[]{:S(2)}) collective-permute-start(bf16[2,96,640]{2,1,0:T(8,128)(2,1)S(1)} %get-tuple-element.176), channel_id=1, source_target_pairs={{0,16},{1,17},{2,18},{3,19},{4,20},{5,21},{6,22},{7,23},{8,24},{9,... | collective-permute-start | bytes 737288 | tf_op jit(solution)/shard_map/ppermute | solution.py:726
  303.6 12.4 %collective-permute-start.30 = (bf16[2,96,640]{2,1,0:T(8,128)(2,1)S(1)}, bf16[2,96,640]{2,1,0:T(8,128)(2,1)S(1)}, u32[]{:S(2)}, u32[]{:S(2)}) collective-permute-start(bf16[2,96,640]{2,1,0:T(8,128)(2,1)S(1)} %get-tuple-element.175), channel_id=1, source_target_pairs={{0,24},{1,25},{2,26},{3,27},{4,28},{5,29},{6,30},{7,31},{8,16},{9,... | collective-permute-start | bytes 737288 | tf_op jit(solution)/shard_map/ppermute | solution.py:726
  316.8 42.6 %collective-permute-start.31 = (bf16[2,96,640]{2,1,0:T(8,128)(2,1)S(1)}, bf16[2,96,640]{2,1,0:T(8,128)(2,1)}, u32[]{:S(2)}, u32[]{:S(2)}) collective-permute-start(bf16[2,96,640]{2,1,0:T(8,128)(2,1)S(1)} %add_convert_fusion.8), channel_id=1, source_target_pairs={{0,2},{1,3},{2,0},{3,1},{4,6},{5,7},{6,4},{7,5},{8,10},{9,11},{10,... | collective-permute-start | bytes 737288 | tf_op jit(solution)/shard_map/ppermute | solution.py:726
  326.1 34.6 %copy-start.11 = (f32[768,768]{1,0:T(8,128)S(1)}, f32[768,768]{1,0:T(8,128)}, u32[]{:S(2)}) copy-start(f32[768,768]{1,0:T(8,128)} %get-tuple-element.147) | copy-start | bytes 7077892
  360.6 3.7 collective-permute-start.33
  364.3 8.0 %collective-permute-start.34 = (bf16[2,96,640]{2,1,0:T(8,128)(2,1)S(1)}, bf16[2,96,640]{2,1,0:T(8,128)(2,1)S(1)}, u32[]{:S(2)}, u32[]{:S(2)}) collective-permute-start(bf16[2,96,640]{2,1,0:T(8,128)(2,1)S(1)} %maximum_select_fusion.4), channel_id=1, source_target_pairs={{0,1},{1,0},{2,3},{3,2},{4,5},{5,4},{6,7},{7,6},{8,9},{9,8},{10,11... | collective-permute-start | bytes 737288 | tf_op jit(solution)/shard_map/ppermute | solution.py:726
  (19 other events, 32.1 us)
Sparse Core Ops, SparseCore 0:
  10.5 75.1 all-gather.5
  159.7 74.2 reduce-scatter.2
  236.5 31.7 reduce-scatter.4
  289.9 53.4 all-gather.3
